TPU v7x, 256 devices: a whole 4x4x8 slice. The times are simulated.
256 devices in a mesh: rows: 32 (over z, y), samp: 8 (over x, core).
Axes of the slice: x: 4, y: 4, z: 8, core: 2. Of those that a mesh axis runs over, the one named last changes fastest.
Arguments:
- coupling_tiles: bfloat16 [512, 32, 128, 128], P('rows', 'samp'), may hold values from -0.09375 to 0.09375
- tile_columns: int32 [512, 32], P('rows', 'samp'), may hold values from 0 to 511, as said below
- sample_matrix: bfloat16 [65536, 512], P('rows'), may hold values from -6 to 6
- phi_leaf: float32 [512, 256], replicated, may hold values from -0.25 to 0.25
- phi_pair: float32 [512, 256], replicated, may hold values from -0.25 to 0.25
- phi_quad: float32 [512, 256], replicated, may hold values from -0.25 to 0.25
Outputs:
- leaf_basis: float32 [65536, 256], P('rows')
- nested_transfer: float32 [8192, 256], P('rows')
- sample_approx: float32 [65536, 512], P('rows', 'samp')
Inputs may be any that keep to these rules, and one draw needn't show every extreme that they name: `tile_columns`: the 32 tile columns of a tile row are distinct and lie in the leaf block of that row or in one of the two leaf blocks beside it (16 tile rows to a leaf block).
All inputs are finite; a program needn't handle non-finite values.
Results may differ from a plain program's by a relative error of at most 0.0003.
Values may be sent and summed in bfloat16 or wider, within the bound.
A program may use at most 128 MiB of HBM per device.

v0:
```python
import jax
import jax.numpy as jnp
from jax import lax
from jax.sharding import PartitionSpec as P

NS_ITERS = 5


HIGH = lax.Precision.HIGHEST


def with_halo(block, sides, width):
    for axis, dim in sides:
        count = lax.axis_size(axis)
        forward = [(i, i + 1) for i in range(count - 1)]
        backward = [(target, source) for source, target in forward]
        low = lax.ppermute(
            lax.slice_in_dim(block, block.shape[dim] - width, None, axis=dim), axis, forward
        )
        high = lax.ppermute(lax.slice_in_dim(block, 0, width, axis=dim), axis, backward)
        block = jnp.concatenate([low, block, high], axis=dim)
    return block


def swapped(value, axis, distance):
    return lax.ppermute(value, axis, [(i, i ^ 1 << distance) for i in range(lax.axis_size(axis))])


def product(left, right):
    return jnp.dot(left, right, precision=HIGH, preferred_element_type=jnp.float32)


def orthogonal(matrix):
    gram_matrix = product(matrix.T, matrix)
    norm_scale = jnp.sqrt(jnp.sum(gram_matrix * gram_matrix)) + 1e-06
    identity = jnp.eye(gram_matrix.shape[0], dtype=jnp.float32)
    iterate = gram_matrix / norm_scale
    inverse_root = identity
    for step in range(NS_ITERS):
        factor = 1.5 * identity - 0.5 * product(inverse_root, iterate)
        iterate = product(iterate, factor)
        inverse_root = product(factor, inverse_root)
    return product(matrix, inverse_root) / jnp.sqrt(norm_scale)


def stack_pair(mine, other, which_bit):
    lower = jnp.where(which_bit == 0, mine, other)
    higher = jnp.where(which_bit == 0, other, mine)
    return jnp.concatenate([lower, higher], axis=0)


def on_device(coupling_tiles, tile_columns, sample_matrix, phi_leaf, phi_pair, phi_quad):
    per_leaf = 16
    leaf_rows = sample_matrix.shape[0]
    sample_cols = sample_matrix.shape[1]
    row_index = lax.axis_index("rows")
    extended = with_halo(sample_matrix, (("rows", 0),), leaf_rows)
    blocks = extended.reshape(3 * per_leaf, leaf_rows // per_leaf, sample_cols)
    local_columns = tile_columns - (row_index - 1) * per_leaf
    picked = jnp.take(blocks, local_columns, axis=0)
    partial_value = jnp.einsum(
        "tkab,tkbs->tas", coupling_tiles, picked, preferred_element_type=jnp.float32
    )
    partial_value = partial_value.reshape(leaf_rows, sample_cols)
    samp_count = lax.axis_size("samp")
    samp_index = lax.axis_index("samp")
    share_cols = sample_cols // samp_count
    sample = lax.psum(partial_value, "samp")

    def sketch(stacked, phi_matrix):
        return product(stacked, phi_matrix)

    def merge_level(stacked, phi_matrix):
        basis_now = orthogonal(sketch(stacked, phi_matrix))
        return (basis_now, product(basis_now.T, stacked))

    basis, coarse = merge_level(sample, phi_leaf)
    sibling_bit = row_index % 2
    cousin_bit = row_index // 2 % 2
    pair = stack_pair(coarse, swapped(coarse, "rows", 0), sibling_bit)
    upper, middle = merge_level(pair, phi_pair)
    quad = stack_pair(middle, swapped(middle, "rows", 1), cousin_bit)
    top, summary = merge_level(quad, phi_quad)
    rank_leaf = coarse.shape[0]
    rank_pair = middle.shape[0]
    own_upper = lax.dynamic_slice_in_dim(upper, sibling_bit * rank_leaf, rank_leaf, 0)
    own_top = lax.dynamic_slice_in_dim(top, cousin_bit * rank_pair, rank_pair, 0)
    nested = product(own_upper, own_top)
    approx = product(
        basis,
        product(nested, lax.dynamic_slice_in_dim(summary, samp_index * share_cols, share_cols, 1)),
    )
    return (basis, nested, approx)


def solution(mesh):
    return jax.shard_map(
        on_device,
        mesh=mesh,
        in_specs=(P("rows", "samp", None, None), P("rows", "samp"), P("rows", None), P(), P(), P()),
        out_specs=(P("rows", None), P("rows", None), P("rows", "samp")),
        check_vma=False,
    )
```

profile of v0, /device:TPU:7, one launch (start us, length us, event | category | flops | bytes accessed | tf_op | source)
XLA Modules:
  0.0 261.3 jit_solution(8823519993755245035)
XLA Ops:
  7.2 4.7 %collective-permute-start = (bf16[2048,512]{1,0:T(8,128)(2,1)}, bf16[2048,512]{1,0:T(8,128)(2,1)}, u32[]{:S(2)}, u32[]{:S(2)}) collective-permute-start(bf16[2048,512]{1,0:T(8,128)(2,1)} %param.8), channel_id=1, source_target_pairs={{0,8},{8,16},{16,24},{24,32},{32,40},{40,48},{48,56},{56,64},{64,7... | collective-permute-start | bytes 6291464 | tf_op jit(solution)/shard_map/ppermute | solution.py:17
  11.9 1.3 collective-permute-start.1
  14.1 41.0 %collective-permute-done = bf16[2048,512]{1,0:T(8,128)(2,1)} collective-permute-done((bf16[2048,512]{1,0:T(8,128)(2,1)}, bf16[2048,512]{1,0:T(8,128)(2,1)}, u32[]{:S(2)}, u32[]{:S(2)}) %collective-permute-start) | collective-permute-done | bytes 2097184 | tf_op jit(solution)/shard_map/ppermute | solution.py:17
  55.2 5.1 %collective-permute-done.1 = bf16[2048,512]{1,0:T(8,128)(2,1)} collective-permute-done((bf16[2048,512]{1,0:T(8,128)(2,1)}, bf16[2048,512]{1,0:T(8,128)(2,1)}, u32[]{:S(2)}, u32[]{:S(2)}) %collective-permute-start.1) | collective-permute-done | bytes 2097184 | tf_op jit(solution)/shard_map/ppermute | solution.py:20
  60.3 6.0 %pad_maximum_fusion = bf16[6144,512]{1,0:T(8,128)(2,1)} fusion(bf16[2048,512]{1,0:T(8,128)(2,1)} %collective-permute-done.1, bf16[2048,512]{1,0:T(8,128)(2,1)} %param.8, bf16[2048,512]{1,0:T(8,128)(2,1)} %collective-permute-done), kind=kLoop, calls=%fused_computation.4 | loop fusion | flops 18874368 | bytes 12582912 | tf_op jit(solution)/shard_map/concatenate | solution.py:21
  66.2 8.3 %gather_fusion = bf16[64,128,512]{2,1,0:T(8,128)(2,1)} fusion(bf16[48,128,512]{2,1,0:T(8,128)(2,1)} %bitcast.104, s32[1024]{0:T(1024)S(1)} %pad_clamp_fusion), kind=kCustom, calls=%fused_computation | custom fusion | bytes 16777472 | tf_op jit(solution)/shard_map/jit(_take)/gather | solution.py:60
  74.5 7.1 %fusion = f32[16,512,128,1]{1,2,3,0:T(8,128)} fusion(bf16[16,4,128,128]{3,2,1,0:T(8,128)(2,1)S(1)} %copy-done, bf16[16,4,128,512]{3,2,1,0:T(8,128)(2,1)} %bitcast.105, pred[16,4]{1,0:T(8,128)(4,1)S(1)} %copy.11), kind=kOutput, calls=%fused_computation.1 | convolution fusion | flops 1077936128 | bytes 14680128 | tf_op jit(solution)/shard_map/tkab,tkbs->tas/dot_general | solution.py:61
  81.7 81.9 %all-reduce.2.cloned.1.call-done = f32[2048,512]{1,0:T(8,128)} async-done(((f32[2048,512]{1,0:T(8,128)}), f32[2048,512]{1,0:T(8,128)}) %all-reduce.2.cloned.1.call-update) | async-done | bytes 4194320 | tf_op jit(solution)/shard_map/psum | solution.py:68
  163.6 5.4 %fusion.26 = f32[2048,256]{1,0:T(8,128)S(1)} fusion(f32[2048,512]{1,0:T(8,128)} %all-reduce.2.cloned.1.call-done, f32[512,256]{1,0:T(8,128)S(1)} %copy-done.11), kind=kOutput, calls=%fused_computation.77 | convolution fusion | flops 3221225472 | bytes 6815744 | tf_op jit(solution)/shard_map/dot_general | solution.py:30
  169.0 1.3 copy-done.1
  170.4 4.2 %multiply_reduce_fusion.2 = (f32[]{:T(128)}, f32[256,256]{1,0:T(8,128)S(1)}) fusion(f32[2048,256]{1,0:T(8,128)S(1)} %fusion.26), kind=kOutput, calls=%fused_computation.50 | convolution fusion | flops 1610743808 | bytes 2359300 | tf_op jit(solution)/shard_map/dot_general | solution.py:30
  180.6 3.7 %convolution_divide_fusion = f32[2048,256]{1,0:T(8,128)S(1)} fusion(f32[2048,256]{1,0:T(8,128)} %copy-done.1, f32[256,256]{1,0:T(8,128)S(1)} %fusion.33, f32[]{:T(128)S(6)} %sqrt.19), kind=kOutput, calls=%fused_computation.6 | convolution fusion | flops 1611137024 | bytes 4456452 | tf_op jit(solution)/shard_map/dot_general | solution.py:30
  184.3 4.0 %fusion.34 = f32[256,512]{1,0:T(8,128)S(1)} fusion(f32[2048,256]{1,0:T(8,128)S(1)} %convolution_divide_fusion, f32[2048,512]{1,0:T(8,128)S(1)} %copy-done.2), kind=kOutput, calls=%fused_computation.85 | convolution fusion | flops 3221225472 | bytes 6815744 | tf_op jit(solution)/shard_map/dot_general | solution.py:30
  188.4 1.3 collective-permute-start.2
  189.7 11.4 %collective-permute-done.2 = f32[256,512]{1,0:T(8,128)} collective-permute-done((f32[256,512]{1,0:T(8,128)S(1)}, f32[256,512]{1,0:T(8,128)}, u32[]{:S(2)}, u32[]{:S(2)}) %collective-permute-start.2) | collective-permute-done | bytes 524320 | tf_op jit(solution)/shard_map/ppermute | solution.py:26
  201.0 1.3 broadcast_select_fusion.3
  202.4 2.0 fusion.7
  205.2 1.6 multiply_reduce_fusion.1
  211.2 1.1 fusion.40
  212.7 1.3 select_subtract_fusion.5
  214.5 1.6 convolution_divide_fusion.2
  216.1 1.9 fusion.6
  218.0 3.0 %collective-permute-start.3 = (f32[256,512]{1,0:T(8,128)}, f32[256,512]{1,0:T(8,128)}, u32[]{:S(2)}, u32[]{:S(2)}) collective-permute-start(f32[256,512]{1,0:T(8,128)} %fusion.6), channel_id=1, source_target_pairs={{0,16},{8,24},{16,0},{24,8},{32,48},{40,56},{48,32},{56,40},{64,80... | collective-permute-start | bytes 1572872 | tf_op jit(solution)/shard_map/ppermute | solution.py:26
  220.9 13.0 %collective-permute-done.3 = f32[256,512]{1,0:T(8,128)} collective-permute-done((f32[256,512]{1,0:T(8,128)}, f32[256,512]{1,0:T(8,128)}, u32[]{:S(2)}, u32[]{:S(2)}) %collective-permute-start.3) | collective-permute-done | bytes 524320 | tf_op jit(solution)/shard_map/ppermute | solution.py:26
  233.9 1.3 broadcast_select_fusion.1
  235.2 2.0 fusion.5
  238.0 1.6 multiply_reduce_fusion
  244.0 1.1 fusion.47
  245.6 1.5 select_subtract_fusion
  247.5 1.6 convolution_divide_fusion.1
  249.1 1.1 fusion.4
  251.0 3.0 %fusion.49 = f32[2048,64]{0,1:T(8,128)} fusion(f32[2048,256]{1,0:T(8,128)S(1)} %copy-done.4, f32[256,64]{1,0:T(8,128)S(1)} %fusion.14), kind=kOutput, calls=%fused_computation.100 | convolution fusion | flops 402653184 | bytes 2686976 | tf_op jit(solution)/shard_map/dot_general | solution.py:30
  (70 shorter events, 17.4 us)
Async XLA Ops:
  7.2 67.4 %copy-start = (bf16[16,4,128,128]{3,2,1,0:T(8,128)(2,1)S(1)}, bf16[16,4,128,128]{3,2,1,0:T(8,128)(2,1)}, u32[]{:S(2)}) copy-start(bf16[16,4,128,128]{3,2,1,0:T(8,128)(2,1)} %param.6) | copy-start | bytes 6291460
  7.2 156.4 %all-reduce.2.cloned.1.call-start = ((), (), s32[]{:S(2)}) async-start(), calls=%async_computation | async-start | bytes 8388608 | tf_op jit(solution)/shard_map/psum | solution.py:68
  7.2 47.9 %collective-permute-start = (bf16[2048,512]{1,0:T(8,128)(2,1)}, bf16[2048,512]{1,0:T(8,128)(2,1)}, u32[]{:S(2)}, u32[]{:S(2)}) collective-permute-start(bf16[2048,512]{1,0:T(8,128)(2,1)} %param.8), channel_id=1, source_target_pairs={{0,8},{8,16},{16,24},{24,32},{32,40},{40,48},{48,56},{56,64},{64,7... | collective-permute-start | bytes 6291464 | tf_op jit(solution)/shard_map/ppermute | solution.py:17
  11.9 48.4 %collective-permute-start.1 = (bf16[2048,512]{1,0:T(8,128)(2,1)}, bf16[2048,512]{1,0:T(8,128)(2,1)}, u32[]{:S(2)}, u32[]{:S(2)}) collective-permute-start(bf16[2048,512]{1,0:T(8,128)(2,1)} %param.8), channel_id=1, source_target_pairs={{8,0},{16,8},{24,16},{32,24},{40,32},{48,40},{56,48},{64,56},{72,6... | collective-permute-start | bytes 6291464 | tf_op jit(solution)/shard_map/ppermute | solution.py:20
  81.6 82.0 %copy-start.11 = (f32[512,256]{1,0:T(8,128)S(1)}, f32[512,256]{1,0:T(8,128)}, u32[]{:S(2)}) copy-start(f32[512,256]{1,0:T(8,128)} %param.9) | copy-start | bytes 1572868
  169.0 1.3 copy-start.1
  180.2 4.1 %copy-start.2 = (f32[2048,512]{1,0:T(8,128)S(1)}, f32[2048,512]{1,0:T(8,128)}, u32[]{:S(2)}) copy-start(f32[2048,512]{1,0:T(8,128)} %all-reduce.2.cloned.1.call-done) | copy-start | bytes 12582916
  184.3 4.1 %copy-start.3 = (f32[2048,256]{1,0:T(8,128)}, f32[2048,256]{1,0:T(8,128)S(1)}, u32[]{:S(2)}) copy-start(f32[2048,256]{1,0:T(8,128)S(1)} %convolution_divide_fusion) | copy-start | bytes 6291460
  188.4 1.3 copy-start.7
  188.4 12.7 %collective-permute-start.2 = (f32[256,512]{1,0:T(8,128)S(1)}, f32[256,512]{1,0:T(8,128)}, u32[]{:S(2)}, u32[]{:S(2)}) collective-permute-start(f32[256,512]{1,0:T(8,128)S(1)} %fusion.34), channel_id=1, source_target_pairs={{0,8},{8,0},{16,24},{24,16},{32,40},{40,32},{48,56},{56,48},{64,72... | collective-permute-start | bytes 1572872 | tf_op jit(solution)/shard_map/ppermute | solution.py:26
  204.4 0.8 copy-start.6
  216.1 1.9 copy-start.8
  218.0 15.9 %collective-permute-start.3 = (f32[256,512]{1,0:T(8,128)}, f32[256,512]{1,0:T(8,128)}, u32[]{:S(2)}, u32[]{:S(2)}) collective-permute-start(f32[256,512]{1,0:T(8,128)} %fusion.6), channel_id=1, source_target_pairs={{0,16},{8,24},{16,0},{24,8},{32,48},{40,56},{48,32},{56,40},{64,80... | collective-permute-start | bytes 1572872 | tf_op jit(solution)/shard_map/ppermute | solution.py:26
  237.2 0.8 copy-start.5
  245.5 4.6 %copy-start.9 = (f32[512,256]{1,0:T(8,128)S(1)}, f32[512,256]{1,0:T(8,128)}, u32[]{:S(2)}) copy-start(f32[512,256]{1,0:T(8,128)} %copy-done.8) | copy-start | bytes 1572868
  245.6 5.5 %copy-start.4 = (f32[2048,256]{1,0:T(8,128)S(1)}, f32[2048,256]{1,0:T(8,128)}, u32[]{:S(2)}) copy-start(f32[2048,256]{1,0:T(8,128)} %copy-done.3) | copy-start | bytes 6291460
  250.6 3.5 %copy-start.10 = (f32[256,256]{1,0:T(8,128)}, f32[256,256]{1,0:T(8,128)S(1)}, u32[]{:S(2)}) copy-start(f32[256,256]{1,0:T(8,128)S(1)} %fusion.8) | copy-start | bytes 786436
Sparse Core Ops, SparseCore 0:
  81.8 81.7 all-reduce.1
where the time goes:
time: 266 us; the launch traced here: 261 us
  waiting for transfers between devices  152 us (57%)
  matrix products  60.6 us (23%)
  between operations  17.3 us (7%)
  local copies, waits for them, and re-layouts  11.5 us (4%)
  starting transfers between devices  10.2 us (4%)
  other arithmetic  9.28 us (3%)
    psum x1, waiting for transfers between devices, on_device(): sample = lax.psum(partial_value, 'samp')  81.9 us
    dot_general x57, matrix products, product(): jnp.dot(left, right, precision=HIGH, preferred_element_type=jnp.float32)  53.5 us
    ppermute x1, waiting for transfers between devices, with_halo(): lax.ppermute(lax.slice_in_dim(block, block.shape[dim] - width, None, axis...  41 us
    ppermute x2, waiting for transfers between devices, swapped(): lax.ppermute(value, axis, [(i, i ^ 1 << distance) for i in range(lax.axis...  24.3 us
    gather x1, local copies, waits for them, and re-layouts, on_device(): picked = jnp.take(blocks, local_columns, axis=0)  8.29 us
    dot_general x1, matrix products, on_device(): jnp.einsum('tkab,tkbs->tas', coupling_tiles, picked, preferred_element_ty...  7.1 us
    concatenate x1, other arithmetic, with_halo(): block = jnp.concatenate([low, block, high], axis=dim)  5.99 us
  transfers between devices with their start and end apart: 5, of which 5 were waited for; matrix products, arithmetic and copies ran while one was open for 0% of the time, Pallas kernels for 0%

commit v1 on v0

v1 whole, which is shorter than its diff:
```python
import functools

import jax
import jax.numpy as jnp
from jax import lax
from jax.experimental import pallas as pl
from jax.experimental.pallas import tpu as pltpu
from jax.sharding import PartitionSpec as P

NS_ITERS = 5
MESH = pl.DeviceIdType.MESH
F32 = jnp.float32
BF16 = jnp.bfloat16
NT, NN = ((1,), (1,)), ((1,), (0,))

N_COPIES = 80
SAMP = 8
CHIPS = 4
RANK = 256
PIECE = RANK // SAMP

SCRATCH = dict(
    ext=pltpu.VMEM((48, 128, 256), BF16),
    tiles=pltpu.VMEM((2, 16, 4, 128, 128), BF16),
    cols_in=pltpu.VMEM((16, 4), jnp.int32),
    cols=pltpu.SMEM((2, 16, 4), jnp.int32),
    phi=pltpu.VMEM((3, 512, 256), F32),
    phi_h=pltpu.VMEM((3, 512, 256), BF16),
    phi_l=pltpu.VMEM((3, 512, 256), BF16),
    part=pltpu.VMEM((4, 4, 128, 256), F32),
    part_in=pltpu.VMEM((3, 4, 128, 256), F32),
    swap=pltpu.VMEM((2, 128, 256), F32),
    samp=pltpu.VMEM((2, 2, 128, 256), F32),
    mine=pltpu.VMEM((3, 256, 256), F32),
    rs_in=pltpu.VMEM((3, 7, PIECE, 256), F32),
    full=pltpu.VMEM((3, 256, 256), F32),
    wpart=pltpu.VMEM((4, 2, 128, 128), F32),
    wrs_in=pltpu.VMEM((7, 128, 128), F32),
    wcol=pltpu.VMEM((2, 128, 128), F32),
    z_all=pltpu.VMEM((SAMP, 2, 256, 256), BF16),
    yx_h=pltpu.VMEM((512, 256), BF16),
    yx_l=pltpu.VMEM((512, 256), BF16),
    f_h=pltpu.VMEM((256, 256), BF16),
    f_l=pltpu.VMEM((256, 256), BF16),
    x_h=pltpu.VMEM((3, 256, 256), BF16),
    x_l=pltpu.VMEM((3, 256, 256), BF16),
    a_h=pltpu.VMEM((6, 256, 256), BF16),
    a_l=pltpu.VMEM((6, 256, 256), BF16),
    t_h=pltpu.VMEM((256, 256), BF16),
    t_l=pltpu.VMEM((256, 256), BF16),
    gram=pltpu.VMEM((2, 256, 256), F32),
    gram_in=pltpu.VMEM((2, 256, 256), F32),
    cross=pltpu.VMEM((256, 256), F32),
    cross_in=pltpu.VMEM((256, 256), F32),
    wc=pltpu.VMEM((2, 256, 128), F32),
    wc_in=pltpu.VMEM((2, 256, 128), F32),
    basis_v=pltpu.VMEM((2048, 256), F32),
    nested_v=pltpu.VMEM((256, 256), F32),
    approx_v=pltpu.VMEM((2048, 64), F32),
    local=pltpu.SemaphoreType.DMA((10,)),
    send=pltpu.SemaphoreType.DMA((N_COPIES,)),
    recv=pltpu.SemaphoreType.DMA((N_COPIES,)),
)


def split(value):
    high = value.astype(BF16)
    return high, (value - high.astype(F32)).astype(BF16)


def dot3(a, b):
    left = jnp.concatenate([a[0], a[0], a[1]], axis=1)
    right = jnp.concatenate([b[0], b[1], b[0]], axis=0)
    return lax.dot_general(left, right, ((NN[0], NN[1]), ((), ())), preferred_element_type=F32)


def kernel(n_rows, *refs):
    tiles_hbm, cols_hbm, b_hbm, phi0_hbm, phi1_hbm, phi2_hbm = refs[:6]
    basis_hbm, nested_hbm, approx_hbm = refs[6:9]
    v = dict(zip(SCRATCH, refs[9:]))

    r = lax.axis_index("rows")
    s = lax.axis_index("samp")
    x = lax.div(s, 2)
    c = lax.rem(s, 2)
    partner = (r, s + 1 - 2 * c)
    left = (lax.rem(r + n_rows - 1, n_rows), s)
    right = (lax.rem(r + 1, n_rows), s)
    sibling = (r + 1 - 2 * lax.rem(r, 2), s)
    cousin = (r + 2 - 4 * lax.rem(lax.div(r, 2), 2), s)

    def samp_peer(offset):
        return lax.rem(s + offset, SAMP)

    def chip_peer(offset):
        return (r, 2 * lax.rem(x + offset, CHIPS) + c)

    barrier = pltpu.get_barrier_semaphore()
    peers = [(r, samp_peer(o)) for o in range(1, SAMP)] + [left, right, cousin]
    for peer in peers:
        pl.semaphore_signal(barrier, inc=1, device_id=peer, device_id_type=MESH)

    locals_ = []

    def local(src, dst):
        copy = pltpu.make_async_copy(src, dst, v["local"].at[len(locals_)])
        locals_.append(copy)
        copy.start()
        return copy

    mine_half = pl.ds(pl.multiple_of(c * 256, 256), 256)
    own_cols = local(cols_hbm, v["cols"].at[0])
    own_tiles = local(tiles_hbm, v["tiles"].at[0])
    own_b = local(b_hbm.at[:, :, mine_half], v["ext"].at[pl.ds(16, 16)])
    phis = [local(p, v["phi"].at[i]) for i, p in enumerate((phi0_hbm, phi1_hbm, phi2_hbm))]
    pl.semaphore_wait(barrier, len(peers))

    sent = []

    def remote(src, dst, device):
        i = len(sent)
        copy = pltpu.make_async_remote_copy(
            src_ref=src,
            dst_ref=dst,
            send_sem=v["send"].at[i],
            recv_sem=v["recv"].at[i],
            device_id=device,
            device_id_type=MESH,
        )
        sent.append(copy)
        copy.start()
        return copy

    with jax.named_scope("halo"):
        halo = [
            remote(b_hbm.at[:, :, mine_half], v["ext"].at[pl.ds(32, 16)], left),
            remote(b_hbm.at[:, :, mine_half], v["ext"].at[pl.ds(0, 16)], right),
        ]
        cols_copy = remote(cols_hbm, v["cols_in"], partner)
        tiles_copy = remote(tiles_hbm, v["tiles"].at[1], partner)
        for i, copy in enumerate(phis):
            copy.wait()
            high, low = split(v["phi"][i])
            v["phi_h"][i] = high
            v["phi_l"][i] = low
        cols_copy.wait_recv()
        other_cols = local(v["cols_in"], v["cols"].at[1])
        for copy in (own_cols, own_tiles, own_b, other_cols):
            copy.wait()
        tiles_copy.wait_recv()
        for copy in halo:
            copy.wait_recv()

    first = (r - 1) * 16

    with jax.named_scope("product"):
        parts = []
        for j, offset in enumerate((2, 1, 3, 0)):
            base = 4 * lax.rem(x + offset, CHIPS)

            def tile_row(t, _, j=j, base=base):
                row = base + t
                lhs = jnp.concatenate(
                    [v["tiles"][h, row, k] for h in range(2) for k in range(4)], axis=1
                )
                rhs = jnp.concatenate(
                    [
                        v["ext"][jnp.clip(v["cols"][h, row, k] - first, 0, 47)]
                        for h in range(2)
                        for k in range(4)
                    ],
                    axis=0,
                )
                v["part"][j, t] = jnp.dot(lhs, rhs, preferred_element_type=F32)
                return 0

            lax.fori_loop(0, 4, tile_row, 0)
            if offset:
                parts.append(
                    remote(v["part"].at[j], v["part_in"].at[offset - 1], chip_peer(offset))
                )
        for copy in parts:
            copy.wait_recv()

        def summed(half):
            at = pl.ds(2 * half, 2)
            total = v["part"][3, at]
            for i in range(3):
                total = total + v["part_in"][i, at]
            return total

        v["swap"][...] = summed(1 - c)
        swapped = remote(v["swap"], v["samp"].at[c], partner)
        v["samp"][c] = summed(c)
        swapped.wait_recv()

    def put(slot, value):
        high, low = split(value)
        v["a_h"][slot] = high
        v["a_l"][slot] = low

    def get(slot):
        return v["a_h"][slot], v["a_l"][slot]

    def phi_of(i):
        return v["phi_h"][i], v["phi_l"][i]

    with jax.named_scope("sums"):
        for half in range(2):
            put(half, v["samp"][half].reshape(256, 256))
        sample = (
            jnp.concatenate([v["a_h"][0], v["a_h"][1]], axis=1),
            jnp.concatenate([v["a_l"][0], v["a_l"][1]], axis=1),
        )
        z = dot3(sample, phi_of(0))
        put(2, z)
        z_high, z_low = split(z)
        v["z_all"][s, 0] = z_high
        v["z_all"][s, 1] = z_low
        t_high, t_low = split(z.T)
        v["t_h"][...] = t_high
        v["t_l"][...] = t_low
        z_t = lambda: (v["t_h"][...], v["t_l"][...])
        v["mine"][0] = dot3(z_t(), get(2))

        def scatter(m):
            return [
                remote(
                    v["mine"].at[m, pl.ds(pl.multiple_of(samp_peer(o) * PIECE, PIECE), PIECE)],
                    v["rs_in"].at[m, o - 1],
                    (r, samp_peer(o)),
                )
                for o in range(1, SAMP)
            ]

        own = pl.ds(pl.multiple_of(s * PIECE, PIECE), PIECE)

        def gather(m, copies):
            for copy in copies:
                copy.wait_recv()
            total = v["mine"][m, own]
            for o in range(SAMP - 1):
                total = total + v["rs_in"][m, o]
            v["full"][m, own] = total
            return [
                remote(v["full"].at[m, own], v["full"].at[m, own], (r, samp_peer(o)))
                for o in range(1, SAMP)
            ]

        scatter_g = scatter(0)
        for half in range(2):
            w = dot3(z_t(), get(half))
            put(3 + half, w)
            for q in range(4):
                v["wpart"][2 * half + q // 2, q % 2] = w[
                    128 * (q % 2) : 128 * (q % 2) + 128, 128 * (q // 2) : 128 * (q // 2) + 128
                ]
        w_all = (
            jnp.concatenate([v["a_h"][3], v["a_h"][4]], axis=1),
            jnp.concatenate([v["a_l"][3], v["a_l"][4]], axis=1),
        )
        v["mine"][1] = dot3(w_all, phi_of(1))
        gather_g = gather(0, scatter_g)
        scatter_n = scatter(1)
        v["mine"][2] = dot3(w_all, phi_of(2))
        gather_n = gather(1, scatter_n)
        scatter_o = scatter(2)
        for copy in gather_g:
            copy.wait_recv()

    eye = jnp.where(
        lax.broadcasted_iota(jnp.int32, (RANK, RANK), 0)
        == lax.broadcasted_iota(jnp.int32, (RANK, RANK), 1),
        F32(1.5),
        F32(0),
    )

    def inverse_root(level, gram):
        norm = jnp.sqrt(jnp.sum(jnp.sum(gram * gram, axis=1, keepdims=True), axis=0, keepdims=True)) + 1e-06
        y = gram / norm
        high, low = split(y)
        factor = split(eye - 0.5 * y)
        new_high, new_low = split(dot3((high, low), factor))
        v["yx_h"][0:256] = new_high
        v["yx_l"][0:256] = new_low
        v["yx_h"][256:512] = factor[0]
        v["yx_l"][256:512] = factor[1]

        def make_factor():
            product = dot3(
                (v["yx_h"][256:512], v["yx_l"][256:512]), (v["yx_h"][0:256], v["yx_l"][0:256])
            )
            high, low = split(eye - 0.5 * product)
            v["f_h"][...] = high
            v["f_l"][...] = low

        def step(_, carry):
            make_factor()
            high, low = split(
                dot3((v["yx_h"][...], v["yx_l"][...]), (v["f_h"][...], v["f_l"][...]))
            )
            v["yx_h"][...] = high
            v["yx_l"][...] = low
            return carry

        lax.fori_loop(0, NS_ITERS - 2, step, 0)
        make_factor()
        high, low = split(
            dot3(
                (v["yx_h"][256:512], v["yx_l"][256:512]), (v["f_h"][...], v["f_l"][...])
            )
        )
        v["x_h"][level] = high
        v["x_l"][level] = low
        return 1.0 / jnp.sqrt(norm)

    def root(level):
        return v["x_h"][level], v["x_l"][level]

    with jax.named_scope("leaf"):
        scale_leaf = inverse_root(0, v["full"][0])
        for copy in gather_n:
            copy.wait_recv()
        put(0, dot3(root(0), split(v["full"][1])) * scale_leaf)
        zp = v["a_h"][0].astype(F32) + v["a_l"][0].astype(F32)
        t_high, t_low = split(zp.T)
        v["t_h"][...] = t_high
        v["t_l"][...] = t_low
        v["gram"][0] = dot3(z_t(), get(0))
        gram_copy = remote(v["gram"].at[0], v["gram_in"].at[0], sibling)

        gather_o = gather(2, scatter_o)
        scatter_w = []
        for o in range(1, SAMP):
            d = samp_peer(o)
            scatter_w.append(
                remote(v["wpart"].at[lax.div(d, 2), lax.rem(d, 2)], v["wrs_in"].at[o - 1], (r, d))
            )
        spread = [
            remote(v["z_all"].at[s], v["z_all"].at[s], chip_peer(o)) for o in range(1, CHIPS)
        ]
        spread_partner = remote(v["z_all"].at[s], v["z_all"].at[s], partner)
        for copy in gather_o:
            copy.wait_recv()
        put(5, dot3(root(0), split(v["full"][2])) * scale_leaf)
        v["cross"][...] = dot3(z_t(), get(5))
        cross_copy = remote(v["cross"], v["cross_in"], sibling)
        gram_copy.wait_recv()

    with jax.named_scope("pair"):
        scale_pair = inverse_root(1, v["gram"][0] + v["gram_in"][0])
        cross_copy.wait_recv()
        zq = dot3(root(1), split(v["cross"][...] + v["cross_in"][...])) * scale_pair
        put(1, zq)
        tq_high, tq_low = split(zq.T)
        v["a_h"][3] = tq_high
        v["a_l"][3] = tq_low
        v["gram"][1] = dot3(get(3), get(1))
        gram_copy = remote(v["gram"].at[1], v["gram_in"].at[1], cousin)

        for copy in scatter_w:
            copy.wait_recv()
        total = v["wpart"][x, c]
        for o in range(SAMP - 1):
            total = total + v["wrs_in"][o]
        v["wcol"][c] = total
        wcol_copy = remote(v["wcol"].at[c], v["wcol"].at[c], partner)
        wcol_copy.wait_recv()
        coarse = dot3(root(0), split(v["wcol"][...].reshape(256, 128))) * scale_leaf
        v["wc"][0] = dot3(z_t(), split(coarse))
        wc_copy = remote(v["wc"].at[0], v["wc_in"].at[0], sibling)
        put(2, dot3(get(0), root(1)) * scale_pair)
        put(4, dot3(get(2), get(1)))
        forwarded = []
        for o in range(1, CHIPS):
            spread[o - 1].wait_recv()
            origin = 2 * lax.rem(x + CHIPS - o, CHIPS) + c
            forwarded.append(remote(v["z_all"].at[origin], v["z_all"].at[origin], partner))
        wc_copy.wait_recv()
        middle = dot3(root(1), split(v["wc"][0] + v["wc_in"][0])) * scale_pair
        v["wc"][1] = dot3(get(3), split(middle))
        wc_copy = remote(v["wc"].at[1], v["wc_in"].at[1], cousin)
        spread_partner.wait_recv()
        for copy in forwarded:
            copy.wait_recv()

        def basis_rows(i, carry):
            rows = pl.ds(pl.multiple_of(i * 256, 256), 256)
            v["basis_v"][rows] = (
                dot3((v["z_all"][i, 0], v["z_all"][i, 1]), root(0)) * scale_leaf
            )
            return carry

        lax.fori_loop(0, SAMP, basis_rows, 0)
        basis_copy = local(v["basis_v"], basis_hbm)
        gram_copy.wait_recv()

    with jax.named_scope("quad"):
        scale_quad = inverse_root(2, v["gram"][1] + v["gram_in"][1])
        nested = dot3(get(4), root(2)) * scale_quad
        v["nested_v"][...] = nested
        nested_copy = local(v["nested_v"], nested_hbm)
        wc_copy.wait_recv()
        summary = dot3(root(2), split(v["wc"][1] + v["wc_in"][1])) * scale_quad
        inner = dot3(split(nested), split(summary))
        inner = jnp.where(c == 0, inner[:, 0:64], inner[:, 64:128])
        put_high, put_low = split(inner)

        def approx_rows(i, carry):
            rows = pl.ds(pl.multiple_of(i * 256, 256), 256)
            v["approx_v"][rows] = dot3(split(v["basis_v"][rows]), (put_high, put_low))
            return carry

        lax.fori_loop(0, SAMP, approx_rows, 0)
        approx_copy = local(v["approx_v"], approx_hbm)
        for copy in (basis_copy, nested_copy, approx_copy):
            copy.wait()
        assert len(sent) <= N_COPIES and len(locals_) <= 10
        for copy in sent:
            copy.wait_send()


def on_device(n_rows, coupling_tiles, tile_columns, sample_matrix, phi_leaf, phi_pair, phi_quad):
    rows = sample_matrix.shape[0]
    any_ = pl.BlockSpec(memory_space=pl.ANY)
    return pl.pallas_call(
        functools.partial(kernel, n_rows),
        out_shape=(
            jax.ShapeDtypeStruct((rows, RANK), F32),
            jax.ShapeDtypeStruct((RANK, RANK), F32),
            jax.ShapeDtypeStruct((rows, sample_matrix.shape[1] // SAMP), F32),
        ),
        in_specs=[any_] * 6,
        out_specs=(any_, any_, any_),
        scratch_shapes=list(SCRATCH.values()),
        compiler_params=pltpu.CompilerParams(
            collective_id=0, has_side_effects=True, vmem_limit_bytes=56 * 2**20
        ),
        name="hss",
    )(coupling_tiles, tile_columns, sample_matrix.reshape(16, 128, 512), phi_leaf, phi_pair, phi_quad)


def solution(mesh):
    return jax.shard_map(
        functools.partial(on_device, mesh.shape["rows"]),
        mesh=mesh,
        in_specs=(P("rows", "samp", None, None), P("rows", "samp"), P("rows", None), P(), P(), P()),
        out_specs=(P("rows", None), P("rows", None), P("rows", "samp")),
        check_vma=False,
    )
```

time: 266 us -> 129 us (0.48)
  the two profiles are of different devices: /device:TPU:7 before, /device:TPU:1 now
where the time goes in v1:
time: 129 us
  Pallas kernels  121 us (94%)
  local copies, waits for them, and re-layouts  7.49 us (6%)
    pallas_call x1, Pallas kernels, on_device(): pl.pallas_call(functools.partial(kernel, n_rows), out_shape=(jax.ShapeDty...  121 us
    unnamed x5, local copies, waits for them, and re-layouts  5.15 us

profile of v1, /device:TPU:1, one launch (start us, length us, event | category | flops | bytes accessed | tf_op | source)
XLA Modules:
  0.0 129.3 jit_solution(6362876836573508873)
XLA Ops:
  0.6 1.4 %copy.9.refs_1_ = s32[16,4]{1,0:T(8,128)} copy(s32[16,4]{0,1:T(4,128)} %param.7) | data formatting | bytes 512 | tf_op args[1]
  2.0 121.1 %hss.1 = (f32[2048,256]{1,0:T(8,128)}, f32[256,256]{1,0:T(8,128)}, f32[2048,64]{1,0:T(8,128)}) custom-call(bf16[16,4,128,128]{3,2,1,0:T(8,128)(2,1)} %refs_0_.1, s32[16,4]{1,0:T(8,128)} %copy.9.refs_1_, bf16[16,128,512]{2,1,0:T(8,128)(2,1)} %bitcast.1, f32[512,256]{1,0:T(8,128)} %refs_3_.1, f32[512,256]{1,0:T(8,128)} %refs_4_.1, f32[512,256]{1,0:T(8,128)} %refs_5_.1), custom_call_target="tpu_custom_call" | custom-call | tf_op jit(solution)/shard_map/hss/pallas_call | solution.py:426
  123.1 2.3 %copy.10 = f32[2048,64]{0,1:T(8,128)} copy(f32[2048,64]{1,0:T(8,128)} %get-tuple-element.5) | data formatting | bytes 1048576 | tf_op jit(solution)/shard_map/hss/pallas_call | solution.py:426
  125.5 0.0 copy-start
  125.5 3.1 %copy.13 = f32[2048,256]{1,0:T(8,128)} copy(f32[2048,256]{1,0:T(8,128)} %get-tuple-element.9) | data formatting | bytes 4194304
  128.6 0.0 copy-done
  128.6 0.7 copy.14
Async XLA Ops:
  125.5 3.1 %copy-start = (f32[256,256]{1,0:T(8,128)S(1)}, f32[256,256]{1,0:T(8,128)}, u32[]{:S(2)}) copy-start(f32[256,256]{1,0:T(8,128)} %get-tuple-element.10) | copy-start | bytes 786436

commit v2 on v1

v2 whole, which is shorter than its diff:
```python
import functools

import jax
import jax.numpy as jnp
from jax import lax
from jax.experimental import pallas as pl
from jax.experimental.pallas import tpu as pltpu
from jax.sharding import PartitionSpec as P

NS_ITERS = 5
MESH = pl.DeviceIdType.MESH
F32 = jnp.float32
BF16 = jnp.bfloat16
NT, NN = ((1,), (1,)), ((1,), (0,))

N_COPIES = 96
SAMP = 8
CHIPS = 4
RANK = 256

I16 = jnp.int16

SCRATCH = dict(
    ext=pltpu.VMEM((48, 128, 256), BF16),
    tiles=pltpu.VMEM((2, 16, 4, 128, 128), BF16),
    cols_in=pltpu.VMEM((4, 16), jnp.int32),
    cols=pltpu.SMEM((2, 4, 16), jnp.int32),
    phi=pltpu.VMEM((3, 512, 256), F32),
    phi_h=pltpu.VMEM((3, 512, 256), BF16),
    phi_l=pltpu.VMEM((3, 512, 256), BF16),
    part=pltpu.VMEM((2, 2, 128, 256), F32),
    code=pltpu.VMEM((6, 256, 256), I16),
    code_in=pltpu.VMEM((6, 256, 256), I16),
    unit=pltpu.VMEM((6, 8, 256), F32),
    unit_in=pltpu.VMEM((6, 8, 256), F32),
    swap=pltpu.VMEM((256, 256), F32),
    samp=pltpu.VMEM((2, 256, 256), F32),
    mine=pltpu.VMEM((3, 256, 256), F32),
    in_core=pltpu.VMEM((3, 128, 256), F32),
    chip=pltpu.VMEM((3, 128, 256), F32),
    in_chip=pltpu.VMEM((3, 128, 256), F32),
    two=pltpu.VMEM((3, 128, 256), F32),
    in_two=pltpu.VMEM((3, 128, 256), F32),
    full=pltpu.VMEM((3, 256, 256), F32),
    wpart=pltpu.VMEM((2, 4, 128, 128), F32),
    w_core=pltpu.VMEM((4, 128, 128), F32),
    w_chip=pltpu.VMEM((4, 128, 128), F32),
    w_in=pltpu.VMEM((3, 128, 128), F32),
    wcol=pltpu.VMEM((2, 128, 128), F32),
    z_own=pltpu.VMEM((2, 256, 256), BF16),
    yx_h=pltpu.VMEM((512, 256), BF16),
    yx_l=pltpu.VMEM((512, 256), BF16),
    f_h=pltpu.VMEM((256, 256), BF16),
    f_l=pltpu.VMEM((256, 256), BF16),
    x_h=pltpu.VMEM((3, 256, 256), BF16),
    x_l=pltpu.VMEM((3, 256, 256), BF16),
    a_h=pltpu.VMEM((6, 256, 256), BF16),
    a_l=pltpu.VMEM((6, 256, 256), BF16),
    t_h=pltpu.VMEM((256, 256), BF16),
    t_l=pltpu.VMEM((256, 256), BF16),
    swapped_pair=pltpu.VMEM((3, 256, 256), F32),
    swapped_in=pltpu.VMEM((3, 128, 256), F32),
    swapped_sum=pltpu.VMEM((3, 256, 256), F32),
    wc=pltpu.VMEM((2, 256, 128), F32),
    wc_in=pltpu.VMEM((2, 256, 128), F32),
    root_v=pltpu.VMEM((2, 256, 256), BF16),
    nested_v=pltpu.VMEM((256, 256), F32),
    inner_t=pltpu.VMEM((128, 256), F32),
    inner_v=pltpu.VMEM((64, 256), F32),
    local=pltpu.SemaphoreType.DMA((12,)),
    send=pltpu.SemaphoreType.DMA((N_COPIES,)),
    recv=pltpu.SemaphoreType.DMA((N_COPIES,)),
)


def split(value):
    high = value.astype(BF16)
    return high, (value - high.astype(F32)).astype(BF16)


def dot3(a, b):
    left = jnp.concatenate([a[0], a[0], a[1]], axis=1)
    right = jnp.concatenate([b[0], b[1], b[0]], axis=0)
    return lax.dot_general(left, right, (NN, ((), ())), preferred_element_type=F32)


def dot3_nt(a, b):
    left = jnp.concatenate([a[0], a[0], a[1]], axis=1)
    right = jnp.concatenate([b[0], b[1], b[0]], axis=1)
    return lax.dot_general(left, right, (NT, ((), ())), preferred_element_type=F32)


def kernel(n_rows, *refs):
    tiles_hbm, cols_hbm, b_hbm, phi0_hbm, phi1_hbm, phi2_hbm = refs[:6]
    z_hbm, root_hbm, nested_hbm, inner_hbm = refs[6:10]
    v = dict(zip(SCRATCH, refs[10:]))

    r = lax.axis_index("rows")
    s = lax.axis_index("samp")
    x = lax.div(s, 2)
    c = lax.rem(s, 2)
    y = lax.rem(r, 4)
    xr, opposite, xl = (lax.rem(x + o, CHIPS) for o in (1, 2, 3))

    def chip(index):
        return (r, 2 * index + c)

    partner = (r, s + 1 - 2 * c)
    left = (lax.rem(r + n_rows - 1, n_rows), s)
    right = (lax.rem(r + 1, n_rows), s)
    sibling = (r + 1 - 2 * lax.rem(r, 2), s)
    cousin = (r + 3 - 2 * y, s)
    first_dim = x + 1 - 2 * lax.rem(x, 2)
    second_dim = 3 - x

    barrier = pltpu.get_barrier_semaphore()
    peers = [partner, chip(xr), chip(opposite), chip(xl), left, right, cousin]
    for peer in peers:
        pl.semaphore_signal(barrier, inc=1, device_id=peer, device_id_type=MESH)

    locals_ = []

    def local(src, dst):
        copy = pltpu.make_async_copy(src, dst, v["local"].at[len(locals_)])
        locals_.append(copy)
        copy.start()
        return copy

    sent = []

    def remote(src, dst, device):
        i = len(sent)
        copy = pltpu.make_async_remote_copy(
            src_ref=src,
            dst_ref=dst,
            send_sem=v["send"].at[i],
            recv_sem=v["recv"].at[i],
            device_id=device,
            device_id_type=MESH,
        )
        sent.append(copy)
        copy.start()
        return copy

    mine_half = pl.ds(pl.multiple_of(c * 256, 256), 256)
    own_cols = local(cols_hbm, v["cols"].at[0])
    pl.semaphore_wait(barrier, len(peers))

    with jax.named_scope("halo"):
        direct = []
        for i in range(4):
            at = 4 * x + i
            piece = b_hbm.at[at, :, mine_half]
            direct.append(
                (
                    remote(piece, v["ext"].at[at], right),
                    remote(piece, v["ext"].at[32 + at], left),
                )
            )
        cols_copy = remote(cols_hbm, v["cols_in"], partner)
        far = pl.ds(4 * opposite, 4)
        far_copies = [
            remote(b_hbm.at[far, :, mine_half], v["ext"].at[far], right),
            remote(b_hbm.at[far, :, mine_half], v["ext"].at[pl.ds(32 + 4 * opposite, 4)], left),
        ]
        tiles_copy = remote(tiles_hbm, v["tiles"].at[1], partner)
        own_tiles = local(tiles_hbm, v["tiles"].at[0])
        own_b = local(b_hbm.at[:, :, mine_half], v["ext"].at[pl.ds(16, 16)])
        phis = [local(p, v["phi"].at[i]) for i, p in enumerate((phi0_hbm, phi1_hbm, phi2_hbm))]
        handed = []
        for i in range(4):
            for side in range(2):
                direct[i][side].wait_recv()
                piece = v["ext"].at[32 * side + 4 * x + i]
                handed.append(remote(piece, piece, chip(xr)))
                handed.append(remote(piece, piece, chip(xl)))
        for i, copy in enumerate(phis):
            copy.wait()
            high, low = split(v["phi"][i])
            v["phi_h"][i] = high
            v["phi_l"][i] = low
        cols_copy.wait_recv()
        other_cols = local(v["cols_in"], v["cols"].at[1])
        for copy in (own_cols, own_tiles, own_b, other_cols):
            copy.wait()
        for copy in [tiles_copy] + far_copies + handed:
            copy.wait_recv()
    first = (r - 1) * 16

    def product(slot, base):
        def tile_row(t, carry):
            row = base + t
            lhs = jnp.concatenate(
                [v["tiles"][h, row, k] for h in range(2) for k in range(4)], axis=1
            )
            rhs = jnp.concatenate(
                [
                    v["ext"][jnp.clip(v["cols"][h, k, row] - first, 0, 47)]
                    for h in range(2)
                    for k in range(4)
                ],
                axis=0,
            )
            v["part"][slot, t] = jnp.dot(lhs, rhs, preferred_element_type=F32)
            return carry

        lax.fori_loop(0, 2, tile_row, 0)
        return v["part"][slot].reshape(256, 256)

    def coded(i, value, device):
        top = jnp.maximum(jnp.max(jnp.abs(value), axis=1, keepdims=True), 1e-30)
        v["code"][i] = jnp.round(value * (32767.0 / top)).astype(jnp.int32).astype(I16)
        v["unit"][i] = jnp.broadcast_to(top * (1 / 32767.0), (256, 128)).T[0:8]
        return (
            remote(v["code"].at[i], v["code_in"].at[i], device),
            remote(v["unit"].at[i], v["unit_in"].at[i], device),
        )

    def decoded(i, copies):
        for copy in copies:
            copy.wait_recv()
        unit = jnp.broadcast_to(v["unit_in"][i, 0:1], (128, 256)).T
        return v["code_in"][i].astype(jnp.int32).astype(F32) * jnp.concatenate([unit, unit], axis=1)

    with jax.named_scope("product"):
        up_far = coded(0, product(0, 4 * opposite), chip(xr))
        down_far = coded(1, product(1, 4 * opposite + 2), chip(xl))
        down_near = coded(2, product(0, 4 * xr + 2), chip(xr))
        up_near = coded(3, product(1, 4 * xl), chip(xl))
        up_sum = coded(4, product(0, 4 * xr) + decoded(0, up_far), chip(xr))
        down_sum = coded(5, product(1, 4 * xl + 2) + decoded(1, down_far), chip(xl))
        product(0, 4 * x)
        product(1, 4 * x + 2)
        upper_in = decoded(3, up_near) + decoded(4, up_sum)
        lower_in = decoded(2, down_near) + decoded(5, down_sum)
        upper_half = v["part"][0].reshape(256, 256) + upper_in
        lower_half = v["part"][1].reshape(256, 256) + lower_in
        v["swap"][...] = jnp.where(c == 0, lower_half, upper_half)
        swapped = remote(v["swap"], v["samp"].at[c], partner)
        v["samp"][c] = jnp.where(c == 0, upper_half, lower_half)
        swapped.wait_recv()
    def put(slot, value):
        high, low = split(value)
        v["a_h"][slot] = high
        v["a_l"][slot] = low

    def get(slot):
        return v["a_h"][slot], v["a_l"][slot]

    def phi_of(i):
        return v["phi_h"][i], v["phi_l"][i]

    def transposed():
        return v["t_h"][...], v["t_l"][...]

    core_rows = pl.ds(pl.multiple_of(c * 128, 128), 128)
    other_rows = pl.ds(pl.multiple_of((1 - c) * 128, 128), 128)

    def sum_core(m):
        return [remote(v["mine"].at[m, other_rows], v["in_core"].at[m], partner)]

    def crossed(ref, into, m, one, two):
        return [
            remote(v[ref].at[m, 0:64], v[into].at[m, 0:64], chip(one)),
            remote(v[ref].at[m, 64:128], v[into].at[m, 64:128], chip(two)),
        ]

    def arrived(copies):
        for copy in copies:
            copy.wait_recv()

    def sum_first(m, copies):
        arrived(copies)
        v["chip"][m] = v["mine"][m, core_rows] + v["in_core"][m]
        return crossed("chip", "in_chip", m, first_dim, second_dim)

    def sum_second(m, copies):
        arrived(copies)
        v["two"][m] = v["chip"][m] + v["in_chip"][m]
        return crossed("two", "in_two", m, second_dim, first_dim)

    def sum_last(m, copies):
        arrived(copies)
        v["full"][m, core_rows] = v["two"][m] + v["in_two"][m]
        return [remote(v["full"].at[m, core_rows], v["full"].at[m, core_rows], partner)]

    with jax.named_scope("sums"):
        for half in range(2):
            put(half, v["samp"][half])
        sample = (
            jnp.concatenate([v["a_h"][0], v["a_h"][1]], axis=1),
            jnp.concatenate([v["a_l"][0], v["a_l"][1]], axis=1),
        )
        z = dot3(sample, phi_of(0))
        z_high, z_low = split(z)
        v["z_own"][0] = z_high
        v["z_own"][1] = z_low
        t_high, t_low = split(z.T)
        v["t_h"][...] = t_high
        v["t_l"][...] = t_low
        v["mine"][0] = dot3(transposed(), (v["z_own"][0], v["z_own"][1]))
        sum_g = sum_core(0)
        z_local = local(v["z_own"], z_hbm.at[s])
        for half in range(2):
            w = dot3(transposed(), get(half))
            put(3 + half, w)
            for q in range(4):
                v["wpart"][q // 2, 2 * half + q % 2] = w[
                    128 * (q // 2) : 128 * (q // 2) + 128, 128 * (q % 2) : 128 * (q % 2) + 128
                ]
        sum_g = sum_first(0, sum_g)
        w_all = (
            jnp.concatenate([v["a_h"][3], v["a_h"][4]], axis=1),
            jnp.concatenate([v["a_l"][3], v["a_l"][4]], axis=1),
        )
        v["mine"][1] = dot3(w_all, phi_of(1))
        sum_n = sum_core(1)
        v["mine"][2] = dot3(w_all, phi_of(2))
        sum_o = sum_core(2)
        w_core = remote(v["wpart"].at[1 - c], v["w_core"], partner)
        sum_n = sum_first(1, sum_n)
        sum_g = sum_second(0, sum_g)
        sum_o = sum_first(2, sum_o)
        sum_n = sum_second(1, sum_n)
        sum_g = sum_last(0, sum_g)
        w_core.wait_recv()
        v["w_chip"][...] = v["wpart"][c] + v["w_core"][...]
        w_copies = [
            remote(v["w_chip"].at[d], v["w_in"].at[o], chip(d))
            for o, d in enumerate((xr, opposite, xl))
        ]
        z_right = remote(v["z_own"], z_hbm.at[s], chip(xr))
        z_left = remote(v["z_own"], z_hbm.at[s], chip(xl))
        z_partner = remote(v["z_own"], z_hbm.at[s], partner)
        sum_o = sum_second(2, sum_o)
        arrived(sum_g)
    eye = jnp.where(
        lax.broadcasted_iota(jnp.int32, (RANK, RANK), 0)
        == lax.broadcasted_iota(jnp.int32, (RANK, RANK), 1),
        F32(1.5),
        F32(0),
    )

    def inverse_root(level, gram):
        norm = (
            jnp.sqrt(
                jnp.sum(jnp.sum(gram * gram, axis=1, keepdims=True), axis=0, keepdims=True)
            )
            + 1e-06
        )
        y0 = gram / norm
        factor = split(eye - 0.5 * y0)
        new_high, new_low = split(dot3(split(y0), factor))
        v["yx_h"][0:256] = new_high
        v["yx_l"][0:256] = new_low
        v["yx_h"][256:512] = factor[0]
        v["yx_l"][256:512] = factor[1]

        def make_factor():
            both = dot3(
                (v["yx_h"][256:512], v["yx_l"][256:512]), (v["yx_h"][0:256], v["yx_l"][0:256])
            )
            high, low = split(eye - 0.5 * both)
            v["f_h"][...] = high
            v["f_l"][...] = low

        def step(_, carry):
            make_factor()
            high, low = split(
                dot3((v["yx_h"][...], v["yx_l"][...]), (v["f_h"][...], v["f_l"][...]))
            )
            v["yx_h"][...] = high
            v["yx_l"][...] = low
            return carry

        lax.fori_loop(0, NS_ITERS - 2, step, 0)
        make_factor()
        result = dot3((v["yx_h"][256:512], v["yx_l"][256:512]), (v["f_h"][...], v["f_l"][...]))
        high, low = split(result)
        v["x_h"][level] = high
        v["x_l"][level] = low
        return 1.0 / jnp.sqrt(norm), result

    def root(level):
        return v["x_h"][level], v["x_l"][level]

    def exchange(i, device):
        return remote(v["swapped_pair"].at[i, core_rows], v["swapped_in"].at[i], device)

    def exchange_core(i, copy):
        copy.wait_recv()
        v["swapped_sum"][i, core_rows] = v["swapped_pair"][i, core_rows] + v["swapped_in"][i]
        return remote(v["swapped_sum"].at[i, core_rows], v["swapped_sum"].at[i, core_rows], partner)

    with jax.named_scope("leaf"):
        scale_leaf, x_leaf = inverse_root(0, v["full"][0])
        sum_n = sum_last(1, sum_n)
        sum_o = sum_last(2, sum_o)
        root_high, root_low = split(x_leaf * scale_leaf)
        v["root_v"][0] = root_high
        v["root_v"][1] = root_low
        root_copy = local(v["root_v"], root_hbm)
        arrived(sum_n)
        zp = dot3(root(0), split(v["full"][1])) * scale_leaf
        put(0, zp)
        t_high, t_low = split(zp.T)
        v["t_h"][...] = t_high
        v["t_l"][...] = t_low
        v["swapped_pair"][0] = dot3(transposed(), get(0))
        gram_copy = exchange(0, sibling)
        arrived(sum_o)
        put(5, dot3(root(0), split(v["full"][2])) * scale_leaf)
        v["swapped_pair"][1] = dot3(transposed(), get(5))
        cross_copy = exchange(1, sibling)
        arrived(w_copies)
        v["wcol"][c] = v["w_chip"][x] + v["w_in"][0] + v["w_in"][1] + v["w_in"][2]
        wcol_copy = remote(v["wcol"].at[c], v["wcol"].at[c], partner)
        gram_copy = exchange_core(0, gram_copy)
        wcol_copy.wait_recv()
        coarse = dot3(root(0), split(v["wcol"][...].reshape(256, 128))) * scale_leaf
        v["wc"][0] = dot3(transposed(), split(coarse))
        wc_copy = remote(v["wc"].at[0], v["wc_in"].at[0], sibling)
        gram_copy.wait_recv()
    with jax.named_scope("pair"):
        scale_pair, _ = inverse_root(1, v["swapped_sum"][0])
        cross_copy = exchange_core(1, cross_copy)
        put(2, dot3(get(0), root(1)) * scale_pair)
        cross_copy.wait_recv()
        zq = dot3(root(1), split(v["swapped_sum"][1])) * scale_pair
        put(1, zq)
        t_high, t_low = split(zq.T)
        v["t_h"][...] = t_high
        v["t_l"][...] = t_low
        v["swapped_pair"][2] = dot3(transposed(), get(1))
        gram_copy = exchange(2, cousin)
        put(4, dot3(get(2), get(1)))
        wc_copy.wait_recv()
        middle = dot3(root(1), split(v["wc"][0] + v["wc_in"][0])) * scale_pair
        v["wc"][1] = dot3(transposed(), split(middle))
        wc_copy = remote(v["wc"].at[1], v["wc_in"].at[1], cousin)
        z_right.wait_recv()
        from_left = 2 * xl + c
        round_right = remote(
            z_hbm.at[from_left, :, 0:128], z_hbm.at[from_left, :, 0:128], chip(xr)
        )
        z_left.wait_recv()
        from_right = 2 * xr + c
        round_left = remote(
            z_hbm.at[from_right, :, 128:256], z_hbm.at[from_right, :, 128:256], chip(xl)
        )
        handed_z = [
            remote(z_hbm.at[from_left], z_hbm.at[from_left], partner),
            remote(z_hbm.at[from_right], z_hbm.at[from_right], partner),
        ]
        gram_copy = exchange_core(2, gram_copy)
        arrived([round_right, round_left])
        from_far = 2 * opposite + c
        handed_z.append(remote(z_hbm.at[from_far], z_hbm.at[from_far], partner))
        gram_copy.wait_recv()
    with jax.named_scope("quad"):
        scale_quad, _ = inverse_root(2, v["swapped_sum"][2])
        nested = dot3(get(4), root(2)) * scale_quad
        v["nested_v"][...] = nested
        nested_copy = local(v["nested_v"], nested_hbm)
        wc_copy.wait_recv()
        summary = dot3(root(2), split(v["wc"][1] + v["wc_in"][1])) * scale_quad
        inner = dot3(split(nested), split(summary))
        v["inner_t"][...] = inner.T
        v["inner_v"][...] = v["inner_t"][pl.ds(pl.multiple_of(c * 64, 64), 64)]
        inner_copy = local(v["inner_v"], inner_hbm)
        arrived([z_partner] + handed_z)
        for copy in (z_local, root_copy, nested_copy, inner_copy):
            copy.wait()
        assert len(sent) <= N_COPIES and len(locals_) <= 12
        for copy in sent:
            copy.wait_send()


def outputs(z_ref, root_ref, nested_ref, inner_ref, basis_out, nested_out, approx_out):
    basis = dot3((z_ref[0, 0], z_ref[0, 1]), (root_ref[0], root_ref[1]))
    basis_out[...] = basis
    approx_out[...] = dot3_nt(split(inner_ref[...]), split(basis))
    nested_out[...] = nested_ref[...]


def on_device(n_rows, coupling_tiles, tile_columns, sample_matrix, phi_leaf, phi_pair, phi_quad):
    rows = sample_matrix.shape[0]
    share = sample_matrix.shape[1] // SAMP
    any_ = pl.BlockSpec(memory_space=pl.ANY)
    z, root, nested, inner = pl.pallas_call(
        functools.partial(kernel, n_rows),
        out_shape=(
            jax.ShapeDtypeStruct((SAMP, 2, RANK, RANK), BF16),
            jax.ShapeDtypeStruct((2, RANK, RANK), BF16),
            jax.ShapeDtypeStruct((RANK, RANK), F32),
            jax.ShapeDtypeStruct((share, RANK), F32),
        ),
        in_specs=[any_] * 6,
        out_specs=(any_,) * 4,
        scratch_shapes=list(SCRATCH.values()),
        compiler_params=pltpu.CompilerParams(
            collective_id=0, has_side_effects=True, vmem_limit_bytes=48 * 2**20
        ),
        name="hss",
    )(
        coupling_tiles,
        tile_columns.T,
        sample_matrix.reshape(16, 128, 512),
        phi_leaf,
        phi_pair,
        phi_quad,
    )
    basis, nested, approx_t = pl.pallas_call(
        outputs,
        grid=(SAMP,),
        out_shape=(
            jax.ShapeDtypeStruct((rows, RANK), F32),
            jax.ShapeDtypeStruct((RANK, RANK), F32),
            jax.ShapeDtypeStruct((share, rows), F32),
        ),
        in_specs=[
            pl.BlockSpec((1, 2, RANK, RANK), lambda i: (i, 0, 0, 0)),
            pl.BlockSpec((2, RANK, RANK), lambda i: (0, 0, 0)),
            pl.BlockSpec((RANK, RANK), lambda i: (0, 0)),
            pl.BlockSpec((share, RANK), lambda i: (0, 0)),
        ],
        out_specs=(
            pl.BlockSpec((RANK, RANK), lambda i: (i, 0)),
            pl.BlockSpec((RANK, RANK), lambda i: (0, 0)),
            pl.BlockSpec((share, RANK), lambda i: (0, i)),
        ),
        compiler_params=pltpu.CompilerParams(vmem_limit_bytes=16 * 2**20),
        name="expand",
    )(z, root, nested, inner)
    return basis, nested, approx_t.T


def solution(mesh):
    return jax.shard_map(
        functools.partial(on_device, mesh.shape["rows"]),
        mesh=mesh,
        in_specs=(P("rows", "samp", None, None), P("rows", "samp"), P("rows", None), P(), P(), P()),
        out_specs=(P("rows", None), P("rows", None), P("rows", "samp")),
        check_vma=False,
    )
```

time: 129 us -> 96.2 us (0.75)
  Pallas kernels: 121 us -> 90.8 us
  local copies, waits for them, and re-layouts: 7.49 us -> 3.8 us
    pallas_call x1, Pallas kernels: 121 us -> 85.1 us  [on_device(): pl.pallas_call(functools.partial(kernel, n_rows), out_shape=(jax.ShapeDty...]
    pallas_call x0 -> x1, Pallas kernels: none -> 5.67 us  [on_device(): pl.pallas_call(outputs, grid=(SAMP,), out_shape=(jax.ShapeDtypeStruct((ro...]
    pallas_call x1 -> x0, local copies, waits for them, and re-layouts: 2.34 us -> none  [on_device(): pl.pallas_call(functools.partial(kernel, n_rows), out_shape=(jax.ShapeDty...]
    unnamed x5 -> x8, local copies, waits for them, and re-layouts: 5.15 us -> 3.8 us
where the time goes in v2:
time: 96.2 us; the launch traced here: 95.3 us
  Pallas kernels  90.8 us (94%)
  local copies, waits for them, and re-layouts  3.8 us (4%)
    pallas_call x1, Pallas kernels, on_device(): pl.pallas_call(functools.partial(kernel, n_rows), out_shape=(jax.ShapeDty...  85.1 us
    pallas_call x1, Pallas kernels, on_device(): pl.pallas_call(outputs, grid=(SAMP,), out_shape=(jax.ShapeDtypeStruct((ro...  5.67 us
    unnamed x8, local copies, waits for them, and re-layouts  3.8 us

profile of v2, /device:TPU:1, one launch (start us, length us, event | category | flops | bytes accessed | tf_op | source)
XLA Modules:
  0.0 95.3 jit_solution(919116893980595038)
XLA Ops:
  0.6 0.0 copy-start
  0.6 1.0 %copy-done = f32[512,256]{1,0:T(8,128)S(1)} copy-done((f32[512,256]{1,0:T(8,128)S(1)}, f32[512,256]{1,0:T(8,128)}, u32[]{:S(2)}) %copy-start) | copy-done | bytes 524312
  1.7 0.0 copy-start.1
  1.7 1.0 %copy-done.1 = f32[512,256]{1,0:T(8,128)S(1)} copy-done((f32[512,256]{1,0:T(8,128)S(1)}, f32[512,256]{1,0:T(8,128)}, u32[]{:S(2)}) %copy-start.1) | copy-done | bytes 524312
  2.7 0.0 copy-start.2
  2.7 1.0 %copy-done.2 = f32[512,256]{1,0:T(8,128)S(1)} copy-done((f32[512,256]{1,0:T(8,128)S(1)}, f32[512,256]{1,0:T(8,128)}, u32[]{:S(2)}) %copy-start.2) | copy-done | bytes 524312
  3.8 0.0 copy-start.3
  3.8 0.7 copy-done.3
  4.4 85.1 %hss.1 = (bf16[8,2,256,256]{3,2,1,0:T(8,128)(2,1)S(1)}, bf16[2,256,256]{2,1,0:T(8,128)(2,1)S(1)}, f32[256,256]{1,0:T(8,128)S(1)}, f32[64,256]{1,0:T(8,128)S(1)}) custom-call(bf16[16,4,128,128]{3,2,1,0:T(8,128)(2,1)} %refs_0_.1, s32[4,16]{1,0:T(4,128)S(1)} %bitcast.3, bf16[16,128,512]{2,1,0:T(8,128)(2,1)} %bitcast.4, f32[512,256]{1,0:T(8,128)S(1)} %copy-done, ...), custom_call_target="tpu_custom_call" | custom-call | tf_op jit(solution)/shard_map/hss/pallas_call | solution.py:490
  89.6 5.7 %expand.1 = (f32[2048,256]{1,0:T(8,128)}, f32[256,256]{1,0:T(8,128)}, f32[64,2048]{1,0:T(8,128)}) custom-call(bf16[8,2,256,256]{3,2,1,0:T(8,128)(2,1)S(1)} %get-tuple-element.10.z_ref, bf16[2,256,256]{2,1,0:T(8,128)(2,1)S(1)} %get-tuple-element.11.root_ref, f32[256,256]{1,0:T(8,128)S(1)} %get-tuple-element.12.nested_ref, ...), custom_call_target="tpu_custom_call" | custom-call | tf_op jit(solution)/shard_map/expand/pallas_call | solution.py:513
Async XLA Ops:
  0.6 1.0 %copy-start = (f32[512,256]{1,0:T(8,128)S(1)}, f32[512,256]{1,0:T(8,128)}, u32[]{:S(2)}) copy-start(f32[512,256]{1,0:T(8,128)} %refs_3_.1) | copy-start | bytes 1572868
  1.7 1.0 %copy-start.1 = (f32[512,256]{1,0:T(8,128)S(1)}, f32[512,256]{1,0:T(8,128)}, u32[]{:S(2)}) copy-start(f32[512,256]{1,0:T(8,128)} %refs_4_.1) | copy-start | bytes 1572868
  2.7 1.0 %copy-start.2 = (f32[512,256]{1,0:T(8,128)S(1)}, f32[512,256]{1,0:T(8,128)}, u32[]{:S(2)}) copy-start(f32[512,256]{1,0:T(8,128)} %refs_5_.1) | copy-start | bytes 1572868
  3.8 0.7 copy-start.3

commit v3 on v2

--- a/solution.py
+++ b/solution.py
@@ -64,9 +64,8 @@
     wc=pltpu.VMEM((2, 256, 128), F32),
     wc_in=pltpu.VMEM((2, 256, 128), F32),
     root_v=pltpu.VMEM((2, 256, 256), BF16),
+    xi_v=pltpu.VMEM((2, 256, 128), BF16),
     nested_v=pltpu.VMEM((256, 256), F32),
-    inner_t=pltpu.VMEM((128, 256), F32),
-    inner_v=pltpu.VMEM((64, 256), F32),
     local=pltpu.SemaphoreType.DMA((12,)),
     send=pltpu.SemaphoreType.DMA((N_COPIES,)),
     recv=pltpu.SemaphoreType.DMA((N_COPIES,)),
@@ -145,7 +144,6 @@
     mine_half = pl.ds(pl.multiple_of(c * 256, 256), 256)
     own_cols = local(cols_hbm, v["cols"].at[0])
     pl.semaphore_wait(barrier, len(peers))
-
     with jax.named_scope("halo"):
         direct = []
         for i in range(4):
@@ -323,15 +321,6 @@
         sum_o = sum_first(2, sum_o)
         sum_n = sum_second(1, sum_n)
         sum_g = sum_last(0, sum_g)
-        w_core.wait_recv()
-        v["w_chip"][...] = v["wpart"][c] + v["w_core"][...]
-        w_copies = [
-            remote(v["w_chip"].at[d], v["w_in"].at[o], chip(d))
-            for o, d in enumerate((xr, opposite, xl))
-        ]
-        z_right = remote(v["z_own"], z_hbm.at[s], chip(xr))
-        z_left = remote(v["z_own"], z_hbm.at[s], chip(xl))
-        z_partner = remote(v["z_own"], z_hbm.at[s], partner)
         sum_o = sum_second(2, sum_o)
         arrived(sum_g)
     eye = jnp.where(
@@ -400,6 +389,12 @@
         v["root_v"][0] = root_high
         v["root_v"][1] = root_low
         root_copy = local(v["root_v"], root_hbm)
+        w_core.wait_recv()
+        v["w_chip"][...] = v["wpart"][c] + v["w_core"][...]
+        w_copies = [
+            remote(v["w_chip"].at[d], v["w_in"].at[o], chip(d))
+            for o, d in enumerate((xr, opposite, xl))
+        ]
         arrived(sum_n)
         zp = dot3(root(0), split(v["full"][1])) * scale_leaf
         put(0, zp)
@@ -408,6 +403,9 @@
         v["t_l"][...] = t_low
         v["swapped_pair"][0] = dot3(transposed(), get(0))
         gram_copy = exchange(0, sibling)
+        z_right = remote(v["z_own"], z_hbm.at[s], chip(xr))
+        z_left = remote(v["z_own"], z_hbm.at[s], chip(xl))
+        z_partner = remote(v["z_own"], z_hbm.at[s], partner)
         arrived(sum_o)
         put(5, dot3(root(0), split(v["full"][2])) * scale_leaf)
         v["swapped_pair"][1] = dot3(transposed(), get(5))
@@ -465,9 +463,12 @@
         wc_copy.wait_recv()
         summary = dot3(root(2), split(v["wc"][1] + v["wc_in"][1])) * scale_quad
         inner = dot3(split(nested), split(summary))
-        v["inner_t"][...] = inner.T
-        v["inner_v"][...] = v["inner_t"][pl.ds(pl.multiple_of(c * 64, 64), 64)]
-        inner_copy = local(v["inner_v"], inner_hbm)
+        inner_high, inner_low = split(
+            dot3((v["root_v"][0], v["root_v"][1]), split(inner))
+        )
+        v["xi_v"][0] = inner_high
+        v["xi_v"][1] = inner_low
+        inner_copy = local(v["xi_v"], inner_hbm)
         arrived([z_partner] + handed_z)
         for copy in (z_local, root_copy, nested_copy, inner_copy):
             copy.wait()
@@ -476,10 +477,14 @@
             copy.wait_send()
 
 
-def outputs(z_ref, root_ref, nested_ref, inner_ref, basis_out, nested_out, approx_out):
-    basis = dot3((z_ref[0, 0], z_ref[0, 1]), (root_ref[0], root_ref[1]))
-    basis_out[...] = basis
-    approx_out[...] = dot3_nt(split(inner_ref[...]), split(basis))
+def outputs(z_ref, root_ref, nested_ref, inner_ref, basis_out, nested_out, approx_out, turned):
+    core = lax.rem(lax.axis_index("samp"), 2)
+    for i in range(2):
+        rows = pl.ds(256 * i, 256)
+        z = z_ref[i, 0], z_ref[i, 1]
+        basis_out[rows] = dot3(z, (root_ref[0], root_ref[1]))
+        turned[i] = dot3(z, (inner_ref[0], inner_ref[1])).T
+        approx_out[:, rows] = turned[i, pl.ds(pl.multiple_of(core * 64, 64), 64)]
     nested_out[...] = nested_ref[...]
 
 
@@ -493,13 +498,13 @@
             jax.ShapeDtypeStruct((SAMP, 2, RANK, RANK), BF16),
             jax.ShapeDtypeStruct((2, RANK, RANK), BF16),
             jax.ShapeDtypeStruct((RANK, RANK), F32),
-            jax.ShapeDtypeStruct((share, RANK), F32),
+            jax.ShapeDtypeStruct((2, RANK, 128), BF16),
         ),
         in_specs=[any_] * 6,
         out_specs=(any_,) * 4,
         scratch_shapes=list(SCRATCH.values()),
         compiler_params=pltpu.CompilerParams(
-            collective_id=0, has_side_effects=True, vmem_limit_bytes=48 * 2**20
+            collective_id=0, has_side_effects=True, vmem_limit_bytes=61 * 2**20
         ),
         name="hss",
     )(
@@ -512,24 +517,25 @@
     )
     basis, nested, approx_t = pl.pallas_call(
         outputs,
-        grid=(SAMP,),
+        grid=(SAMP // 2,),
         out_shape=(
             jax.ShapeDtypeStruct((rows, RANK), F32),
             jax.ShapeDtypeStruct((RANK, RANK), F32),
             jax.ShapeDtypeStruct((share, rows), F32),
         ),
         in_specs=[
-            pl.BlockSpec((1, 2, RANK, RANK), lambda i: (i, 0, 0, 0)),
+            pl.BlockSpec((2, 2, RANK, RANK), lambda i: (i, 0, 0, 0)),
             pl.BlockSpec((2, RANK, RANK), lambda i: (0, 0, 0)),
             pl.BlockSpec((RANK, RANK), lambda i: (0, 0)),
-            pl.BlockSpec((share, RANK), lambda i: (0, 0)),
+            pl.BlockSpec((2, RANK, 128), lambda i: (0, 0, 0)),
         ],
         out_specs=(
-            pl.BlockSpec((RANK, RANK), lambda i: (i, 0)),
+            pl.BlockSpec((2 * RANK, RANK), lambda i: (i, 0)),
             pl.BlockSpec((RANK, RANK), lambda i: (0, 0)),
-            pl.BlockSpec((share, RANK), lambda i: (0, i)),
+            pl.BlockSpec((share, 2 * RANK), lambda i: (0, i)),
         ),
-        compiler_params=pltpu.CompilerParams(vmem_limit_bytes=16 * 2**20),
+        scratch_shapes=[pltpu.VMEM((2, 128, RANK), F32)],
+        compiler_params=pltpu.CompilerParams(vmem_limit_bytes=61 * 2**20),
         name="expand",
     )(z, root, nested, inner)
     return basis, nested, approx_t.T

time: 96.2 us -> 86.7 us (0.901)
  Pallas kernels: 90.8 us -> 85.1 us
  local copies, waits for them, and re-layouts: 3.8 us -> 0 us
    pallas_call x1, Pallas kernels: 85.1 us -> 79.8 us  [on_device(): pl.pallas_call(functools.partial(kernel, n_rows), out_shape=(jax.ShapeDty...]
    unnamed x8 -> x0, local copies, waits for them, and re-layouts: 3.8 us -> none
where the time goes in v3:
time: 86.7 us; the launch traced here: 85.7 us
  Pallas kernels  85.1 us (98%)
    pallas_call x1, Pallas kernels, on_device(): pl.pallas_call(functools.partial(kernel, n_rows), out_shape=(jax.ShapeDty...  79.8 us
    pallas_call x1, Pallas kernels, on_device(): pl.pallas_call(outputs, grid=(SAMP // 2,), out_shape=(jax.ShapeDtypeStruc...  5.26 us

profile of v3, /device:TPU:1, one launch (start us, length us, event | category | flops | bytes accessed | tf_op | source)
XLA Modules:
  0.0 85.7 jit_solution(7901318461114058767)
XLA Ops:
  0.6 79.8 %hss.1 = (bf16[8,2,256,256]{3,2,1,0:T(8,128)(2,1)}, bf16[2,256,256]{2,1,0:T(8,128)(2,1)}, f32[256,256]{1,0:T(8,128)}, bf16[2,256,128]{2,1,0:T(8,128)(2,1)}) custom-call(bf16[16,4,128,128]{3,2,1,0:T(8,128)(2,1)} %refs_0_.1, s32[4,16]{1,0:T(4,128)} %bitcast.4, bf16[16,128,512]{2,1,0:T(8,128)(2,1)} %bitcast.3, f32[512,256]{1,0:T(8,128)} %refs_3_.1, ...), custom_call_target="tpu_custom_call" | custom-call | tf_op jit(solution)/shard_map/hss/pallas_call | solution.py:495
  80.5 5.3 %expand.1 = (f32[2048,256]{1,0:T(8,128)}, f32[256,256]{1,0:T(8,128)}, f32[64,2048]{1,0:T(8,128)}) custom-call(bf16[8,2,256,256]{3,2,1,0:T(8,128)(2,1)} %get-tuple-element.10.z_ref, bf16[2,256,256]{2,1,0:T(8,128)(2,1)} %get-tuple-element.11.root_ref, f32[256,256]{1,0:T(8,128)} %get-tuple-element.12.nested_ref, bf16[2,256,128]{2,1,0:T(8,128)(2,1)} %get-tuple-element.13.inner_ref), custom_call_target="tpu_custom_call" | custom-call | tf_op jit(solution)/shard_map/expand/pallas_call | solution.py:518

commit v4 on v3

--- a/solution.py
+++ b/solution.py
@@ -320,8 +320,14 @@
         sum_g = sum_second(0, sum_g)
         sum_o = sum_first(2, sum_o)
         sum_n = sum_second(1, sum_n)
+        sum_o = sum_second(2, sum_o)
         sum_g = sum_last(0, sum_g)
-        sum_o = sum_second(2, sum_o)
+        w_core.wait_recv()
+        v["w_chip"][...] = v["wpart"][c] + v["w_core"][...]
+        w_copies = [
+            remote(v["w_chip"].at[d], v["w_in"].at[o], chip(d))
+            for o, d in enumerate((xr, opposite, xl))
+        ]
         arrived(sum_g)
     eye = jnp.where(
         lax.broadcasted_iota(jnp.int32, (RANK, RANK), 0)
@@ -330,7 +336,7 @@
         F32(0),
     )
 
-    def inverse_root(level, gram):
+    def inverse_root(level, gram, meanwhile):
         norm = (
             jnp.sqrt(
                 jnp.sum(jnp.sum(gram * gram, axis=1, keepdims=True), axis=0, keepdims=True)
@@ -362,13 +368,15 @@
             v["yx_l"][...] = low
             return carry
 
-        lax.fori_loop(0, NS_ITERS - 2, step, 0)
+        step(0, 0)
+        passed_on = meanwhile()
+        lax.fori_loop(0, NS_ITERS - 3, step, 0)
         make_factor()
         result = dot3((v["yx_h"][256:512], v["yx_l"][256:512]), (v["f_h"][...], v["f_l"][...]))
         high, low = split(result)
         v["x_h"][level] = high
         v["x_l"][level] = low
-        return 1.0 / jnp.sqrt(norm), result
+        return 1.0 / jnp.sqrt(norm), result, passed_on
 
     def root(level):
         return v["x_h"][level], v["x_l"][level]
@@ -382,19 +390,9 @@
         return remote(v["swapped_sum"].at[i, core_rows], v["swapped_sum"].at[i, core_rows], partner)
 
     with jax.named_scope("leaf"):
-        scale_leaf, x_leaf = inverse_root(0, v["full"][0])
-        sum_n = sum_last(1, sum_n)
-        sum_o = sum_last(2, sum_o)
-        root_high, root_low = split(x_leaf * scale_leaf)
-        v["root_v"][0] = root_high
-        v["root_v"][1] = root_low
-        root_copy = local(v["root_v"], root_hbm)
-        w_core.wait_recv()
-        v["w_chip"][...] = v["wpart"][c] + v["w_core"][...]
-        w_copies = [
-            remote(v["w_chip"].at[d], v["w_in"].at[o], chip(d))
-            for o, d in enumerate((xr, opposite, xl))
-        ]
+        scale_leaf, x_leaf, (sum_n, sum_o) = inverse_root(
+            0, v["full"][0], lambda: (sum_last(1, sum_n), sum_last(2, sum_o))
+        )
         arrived(sum_n)
         zp = dot3(root(0), split(v["full"][1])) * scale_leaf
         put(0, zp)
@@ -403,25 +401,30 @@
         v["t_l"][...] = t_low
         v["swapped_pair"][0] = dot3(transposed(), get(0))
         gram_copy = exchange(0, sibling)
-        z_right = remote(v["z_own"], z_hbm.at[s], chip(xr))
-        z_left = remote(v["z_own"], z_hbm.at[s], chip(xl))
-        z_partner = remote(v["z_own"], z_hbm.at[s], partner)
         arrived(sum_o)
         put(5, dot3(root(0), split(v["full"][2])) * scale_leaf)
         v["swapped_pair"][1] = dot3(transposed(), get(5))
         cross_copy = exchange(1, sibling)
+        z_right = remote(v["z_own"], z_hbm.at[s], chip(xr))
+        z_left = remote(v["z_own"], z_hbm.at[s], chip(xl))
+        z_partner = remote(v["z_own"], z_hbm.at[s], partner)
+        root_high, root_low = split(x_leaf * scale_leaf)
+        v["root_v"][0] = root_high
+        v["root_v"][1] = root_low
+        root_copy = local(v["root_v"], root_hbm)
+        gram_copy = exchange_core(0, gram_copy)
         arrived(w_copies)
         v["wcol"][c] = v["w_chip"][x] + v["w_in"][0] + v["w_in"][1] + v["w_in"][2]
         wcol_copy = remote(v["wcol"].at[c], v["wcol"].at[c], partner)
-        gram_copy = exchange_core(0, gram_copy)
         wcol_copy.wait_recv()
         coarse = dot3(root(0), split(v["wcol"][...].reshape(256, 128))) * scale_leaf
         v["wc"][0] = dot3(transposed(), split(coarse))
         wc_copy = remote(v["wc"].at[0], v["wc_in"].at[0], sibling)
         gram_copy.wait_recv()
     with jax.named_scope("pair"):
-        scale_pair, _ = inverse_root(1, v["swapped_sum"][0])
-        cross_copy = exchange_core(1, cross_copy)
+        scale_pair, _, cross_copy = inverse_root(
+            1, v["swapped_sum"][0], lambda: exchange_core(1, cross_copy)
+        )
         put(2, dot3(get(0), root(1)) * scale_pair)
         cross_copy.wait_recv()
         zq = dot3(root(1), split(v["swapped_sum"][1])) * scale_pair
@@ -451,12 +454,15 @@
             remote(z_hbm.at[from_right], z_hbm.at[from_right], partner),
         ]
         gram_copy = exchange_core(2, gram_copy)
-        arrived([round_right, round_left])
-        from_far = 2 * opposite + c
-        handed_z.append(remote(z_hbm.at[from_far], z_hbm.at[from_far], partner))
         gram_copy.wait_recv()
     with jax.named_scope("quad"):
-        scale_quad, _ = inverse_root(2, v["swapped_sum"][2])
+        def far_z():
+            arrived([round_right, round_left])
+            from_far = 2 * opposite + c
+            return remote(z_hbm.at[from_far], z_hbm.at[from_far], partner)
+
+        scale_quad, _, far_copy = inverse_root(2, v["swapped_sum"][2], far_z)
+        handed_z.append(far_copy)
         nested = dot3(get(4), root(2)) * scale_quad
         v["nested_v"][...] = nested
         nested_copy = local(v["nested_v"], nested_hbm)

time: 86.7 us -> 88.8 us (1.024)
  Pallas kernels: 85.1 us -> 88 us
    pallas_call x1, Pallas kernels: 79.8 us -> 82.7 us  [on_device(): pl.pallas_call(functools.partial(kernel, n_rows), out_shape=(jax.ShapeDty...]
where the time goes in v4:
time: 88.8 us; the launch traced here: 88.6 us
  Pallas kernels  88 us (99%)
    pallas_call x1, Pallas kernels, on_device(): pl.pallas_call(functools.partial(kernel, n_rows), out_shape=(jax.ShapeDty...  82.7 us
    pallas_call x1, Pallas kernels, on_device(): pl.pallas_call(outputs, grid=(SAMP // 2,), out_shape=(jax.ShapeDtypeStruc...  5.26 us

profile of v4, /device:TPU:1, one launch (start us, length us, event | category | flops | bytes accessed | tf_op | source)
XLA Modules:
  0.0 88.6 jit_solution(14835865576788209690)
XLA Ops:
  0.6 82.7 %hss.1 = (bf16[8,2,256,256]{3,2,1,0:T(8,128)(2,1)}, bf16[2,256,256]{2,1,0:T(8,128)(2,1)}, f32[256,256]{1,0:T(8,128)}, bf16[2,256,128]{2,1,0:T(8,128)(2,1)}) custom-call(bf16[16,4,128,128]{3,2,1,0:T(8,128)(2,1)} %refs_0_.1, s32[4,16]{1,0:T(4,128)} %bitcast.4, bf16[16,128,512]{2,1,0:T(8,128)(2,1)} %bitcast.3, f32[512,256]{1,0:T(8,128)} %refs_3_.1, ...), custom_call_target="tpu_custom_call" | custom-call | tf_op jit(solution)/shard_map/hss/pallas_call | solution.py:501
  83.3 5.3 %expand.1 = (f32[2048,256]{1,0:T(8,128)}, f32[256,256]{1,0:T(8,128)}, f32[64,2048]{1,0:T(8,128)}) custom-call(bf16[8,2,256,256]{3,2,1,0:T(8,128)(2,1)} %get-tuple-element.10.z_ref, bf16[2,256,256]{2,1,0:T(8,128)(2,1)} %get-tuple-element.11.root_ref, f32[256,256]{1,0:T(8,128)} %get-tuple-element.12.nested_ref, bf16[2,256,128]{2,1,0:T(8,128)(2,1)} %get-tuple-element.13.inner_ref), custom_call_target="tpu_custom_call" | custom-call | tf_op jit(solution)/shard_map/expand/pallas_call | solution.py:524

commit v5 on v4

--- a/solution.py
+++ b/solution.py
@@ -324,10 +324,6 @@
         sum_g = sum_last(0, sum_g)
         w_core.wait_recv()
         v["w_chip"][...] = v["wpart"][c] + v["w_core"][...]
-        w_copies = [
-            remote(v["w_chip"].at[d], v["w_in"].at[o], chip(d))
-            for o, d in enumerate((xr, opposite, xl))
-        ]
         arrived(sum_g)
     eye = jnp.where(
         lax.broadcasted_iota(jnp.int32, (RANK, RANK), 0)
@@ -390,9 +386,16 @@
         return remote(v["swapped_sum"].at[i, core_rows], v["swapped_sum"].at[i, core_rows], partner)
 
     with jax.named_scope("leaf"):
-        scale_leaf, x_leaf, (sum_n, sum_o) = inverse_root(
-            0, v["full"][0], lambda: (sum_last(1, sum_n), sum_last(2, sum_o))
-        )
+
+        def last_sums():
+            last_n, last_o = sum_last(1, sum_n), sum_last(2, sum_o)
+            columns = [
+                remote(v["w_chip"].at[d], v["w_in"].at[o], chip(d))
+                for o, d in enumerate((xr, opposite, xl))
+            ]
+            return last_n, last_o, columns
+
+        scale_leaf, x_leaf, (sum_n, sum_o, w_copies) = inverse_root(0, v["full"][0], last_sums)
         arrived(sum_n)
         zp = dot3(root(0), split(v["full"][1])) * scale_leaf
         put(0, zp)
@@ -401,13 +404,13 @@
         v["t_l"][...] = t_low
         v["swapped_pair"][0] = dot3(transposed(), get(0))
         gram_copy = exchange(0, sibling)
+        z_right = remote(v["z_own"], z_hbm.at[s], chip(xr))
+        z_left = remote(v["z_own"], z_hbm.at[s], chip(xl))
+        z_partner = remote(v["z_own"], z_hbm.at[s], partner)
         arrived(sum_o)
         put(5, dot3(root(0), split(v["full"][2])) * scale_leaf)
         v["swapped_pair"][1] = dot3(transposed(), get(5))
         cross_copy = exchange(1, sibling)
-        z_right = remote(v["z_own"], z_hbm.at[s], chip(xr))
-        z_left = remote(v["z_own"], z_hbm.at[s], chip(xl))
-        z_partner = remote(v["z_own"], z_hbm.at[s], partner)
         root_high, root_low = split(x_leaf * scale_leaf)
         v["root_v"][0] = root_high
         v["root_v"][1] = root_low
@@ -456,13 +459,10 @@
         gram_copy = exchange_core(2, gram_copy)
         gram_copy.wait_recv()
     with jax.named_scope("quad"):
-        def far_z():
-            arrived([round_right, round_left])
-            from_far = 2 * opposite + c
-            return remote(z_hbm.at[from_far], z_hbm.at[from_far], partner)
-
-        scale_quad, _, far_copy = inverse_root(2, v["swapped_sum"][2], far_z)
-        handed_z.append(far_copy)
+        scale_quad, _, _ = inverse_root(2, v["swapped_sum"][2], lambda: None)
+        arrived([round_right, round_left])
+        from_far = 2 * opposite + c
+        handed_z.append(remote(z_hbm.at[from_far], z_hbm.at[from_far], partner))
         nested = dot3(get(4), root(2)) * scale_quad
         v["nested_v"][...] = nested
         nested_copy = local(v["nested_v"], nested_hbm)

time: 88.8 us -> 86.3 us (0.972)
  Pallas kernels: 88 us -> 84.7 us
    pallas_call x1, Pallas kernels: 82.7 us -> 79.5 us  [on_device(): pl.pallas_call(functools.partial(kernel, n_rows), out_shape=(jax.ShapeDty...]
where the time goes in v5:
time: 86.3 us; the launch traced here: 85.4 us
  Pallas kernels  84.7 us (98%)
    pallas_call x1, Pallas kernels, on_device(): pl.pallas_call(functools.partial(kernel, n_rows), out_shape=(jax.ShapeDty...  79.5 us
    pallas_call x1, Pallas kernels, on_device(): pl.pallas_call(outputs, grid=(SAMP // 2,), out_shape=(jax.ShapeDtypeStruc...  5.26 us

profile of v5, /device:TPU:1, one launch (start us, length us, event | category | flops | bytes accessed | tf_op | source)
XLA Modules:
  0.0 85.4 jit_solution(16514812867284557150)
XLA Ops:
  0.6 79.5 %hss.1 = (bf16[8,2,256,256]{3,2,1,0:T(8,128)(2,1)}, bf16[2,256,256]{2,1,0:T(8,128)(2,1)}, f32[256,256]{1,0:T(8,128)}, bf16[2,256,128]{2,1,0:T(8,128)(2,1)}) custom-call(bf16[16,4,128,128]{3,2,1,0:T(8,128)(2,1)} %refs_0_.1, s32[4,16]{1,0:T(4,128)} %bitcast.4, bf16[16,128,512]{2,1,0:T(8,128)(2,1)} %bitcast.3, f32[512,256]{1,0:T(8,128)} %refs_3_.1, ...), custom_call_target="tpu_custom_call" | custom-call | tf_op jit(solution)/shard_map/hss/pallas_call | solution.py:501
  80.1 5.3 %expand.1 = (f32[2048,256]{1,0:T(8,128)}, f32[256,256]{1,0:T(8,128)}, f32[64,2048]{1,0:T(8,128)}) custom-call(bf16[8,2,256,256]{3,2,1,0:T(8,128)(2,1)} %get-tuple-element.10.z_ref, bf16[2,256,256]{2,1,0:T(8,128)(2,1)} %get-tuple-element.11.root_ref, f32[256,256]{1,0:T(8,128)} %get-tuple-element.12.nested_ref, bf16[2,256,128]{2,1,0:T(8,128)(2,1)} %get-tuple-element.13.inner_ref), custom_call_target="tpu_custom_call" | custom-call | tf_op jit(solution)/shard_map/expand/pallas_call | solution.py:524

commit v6 on v5

--- a/solution.py
+++ b/solution.py
@@ -251,16 +251,31 @@
     def transposed():
         return v["t_h"][...], v["t_l"][...]
 
-    core_rows = pl.ds(pl.multiple_of(c * 128, 128), 128)
-    other_rows = pl.ds(pl.multiple_of((1 - c) * 128, 128), 128)
+    def packed(gram):
+        corner = jnp.concatenate([gram[128:192, 128:256], gram[192:256, 128:256]], axis=1)
+        return jnp.concatenate([gram[0:128], corner], axis=0)
+
+    def unpacked(rows):
+        corner = jnp.concatenate([rows[128:192, 0:128], rows[128:192, 128:256]], axis=0)
+        low = jnp.concatenate([rows[0:128, 128:256].T, corner], axis=1)
+        return jnp.concatenate([rows[0:128], low], axis=0)
+
+    def core_rows(size, core):
+        return pl.ds(pl.multiple_of(core * size, size), size)
+
+    def half_of(m):
+        return 96 if m == 0 else 128
 
     def sum_core(m):
-        return [remote(v["mine"].at[m, other_rows], v["in_core"].at[m], partner)]
+        size = half_of(m)
+        rows = core_rows(size, 1 - c)
+        return [remote(v["mine"].at[m, rows], v["in_core"].at[m, 0:size], partner)]
 
     def crossed(ref, into, m, one, two):
+        size, cut = half_of(m), half_of(m) // 2
         return [
-            remote(v[ref].at[m, 0:64], v[into].at[m, 0:64], chip(one)),
-            remote(v[ref].at[m, 64:128], v[into].at[m, 64:128], chip(two)),
+            remote(v[ref].at[m, 0:cut], v[into].at[m, 0:cut], chip(one)),
+            remote(v[ref].at[m, cut:size], v[into].at[m, cut:size], chip(two)),
         ]
 
     def arrived(copies):
@@ -269,18 +284,22 @@
 
     def sum_first(m, copies):
         arrived(copies)
-        v["chip"][m] = v["mine"][m, core_rows] + v["in_core"][m]
+        size = half_of(m)
+        v["chip"][m, 0:size] = v["mine"][m, core_rows(size, c)] + v["in_core"][m, 0:size]
         return crossed("chip", "in_chip", m, first_dim, second_dim)
 
     def sum_second(m, copies):
         arrived(copies)
-        v["two"][m] = v["chip"][m] + v["in_chip"][m]
+        size = half_of(m)
+        v["two"][m, 0:size] = v["chip"][m, 0:size] + v["in_chip"][m, 0:size]
         return crossed("two", "in_two", m, second_dim, first_dim)
 
     def sum_last(m, copies):
         arrived(copies)
-        v["full"][m, core_rows] = v["two"][m] + v["in_two"][m]
-        return [remote(v["full"].at[m, core_rows], v["full"].at[m, core_rows], partner)]
+        size = half_of(m)
+        rows = core_rows(size, c)
+        v["full"][m, rows] = v["two"][m, 0:size] + v["in_two"][m, 0:size]
+        return [remote(v["full"].at[m, rows], v["full"].at[m, rows], partner)]
 
     with jax.named_scope("sums"):
         for half in range(2):
@@ -296,7 +315,7 @@
         t_high, t_low = split(z.T)
         v["t_h"][...] = t_high
         v["t_l"][...] = t_low
-        v["mine"][0] = dot3(transposed(), (v["z_own"][0], v["z_own"][1]))
+        v["mine"][0, 0:192] = packed(dot3(transposed(), (v["z_own"][0], v["z_own"][1])))
         sum_g = sum_core(0)
         z_local = local(v["z_own"], z_hbm.at[s])
         for half in range(2):
@@ -378,12 +397,16 @@
         return v["x_h"][level], v["x_l"][level]
 
     def exchange(i, device):
-        return remote(v["swapped_pair"].at[i, core_rows], v["swapped_in"].at[i], device)
+        size = 128 if i == 1 else 96
+        rows = core_rows(size, c)
+        return remote(v["swapped_pair"].at[i, rows], v["swapped_in"].at[i, 0:size], device)
 
     def exchange_core(i, copy):
         copy.wait_recv()
-        v["swapped_sum"][i, core_rows] = v["swapped_pair"][i, core_rows] + v["swapped_in"][i]
-        return remote(v["swapped_sum"].at[i, core_rows], v["swapped_sum"].at[i, core_rows], partner)
+        size = 128 if i == 1 else 96
+        rows = core_rows(size, c)
+        v["swapped_sum"][i, rows] = v["swapped_pair"][i, rows] + v["swapped_in"][i, 0:size]
+        return remote(v["swapped_sum"].at[i, rows], v["swapped_sum"].at[i, rows], partner)
 
     with jax.named_scope("leaf"):
 
@@ -395,14 +418,14 @@
             ]
             return last_n, last_o, columns
 
-        scale_leaf, x_leaf, (sum_n, sum_o, w_copies) = inverse_root(0, v["full"][0], last_sums)
+        scale_leaf, x_leaf, (sum_n, sum_o, w_copies) = inverse_root(0, unpacked(v["full"][0, 0:192]), last_sums)
         arrived(sum_n)
         zp = dot3(root(0), split(v["full"][1])) * scale_leaf
         put(0, zp)
         t_high, t_low = split(zp.T)
         v["t_h"][...] = t_high
         v["t_l"][...] = t_low
-        v["swapped_pair"][0] = dot3(transposed(), get(0))
+        v["swapped_pair"][0, 0:192] = packed(dot3(transposed(), get(0)))
         gram_copy = exchange(0, sibling)
         z_right = remote(v["z_own"], z_hbm.at[s], chip(xr))
         z_left = remote(v["z_own"], z_hbm.at[s], chip(xl))
@@ -426,7 +449,7 @@
         gram_copy.wait_recv()
     with jax.named_scope("pair"):
         scale_pair, _, cross_copy = inverse_root(
-            1, v["swapped_sum"][0], lambda: exchange_core(1, cross_copy)
+            1, unpacked(v["swapped_sum"][0, 0:192]), lambda: exchange_core(1, cross_copy)
         )
         put(2, dot3(get(0), root(1)) * scale_pair)
         cross_copy.wait_recv()
@@ -435,7 +458,7 @@
         t_high, t_low = split(zq.T)
         v["t_h"][...] = t_high
         v["t_l"][...] = t_low
-        v["swapped_pair"][2] = dot3(transposed(), get(1))
+        v["swapped_pair"][2, 0:192] = packed(dot3(transposed(), get(1)))
         gram_copy = exchange(2, cousin)
         put(4, dot3(get(2), get(1)))
         wc_copy.wait_recv()
@@ -459,7 +482,7 @@
         gram_copy = exchange_core(2, gram_copy)
         gram_copy.wait_recv()
     with jax.named_scope("quad"):
-        scale_quad, _, _ = inverse_root(2, v["swapped_sum"][2], lambda: None)
+        scale_quad, _, _ = inverse_root(2, unpacked(v["swapped_sum"][2, 0:192]), lambda: None)
         arrived([round_right, round_left])
         from_far = 2 * opposite + c
         handed_z.append(remote(z_hbm.at[from_far], z_hbm.at[from_far], partner))
@@ -510,7 +533,7 @@
         out_specs=(any_,) * 4,
         scratch_shapes=list(SCRATCH.values()),
         compiler_params=pltpu.CompilerParams(
-            collective_id=0, has_side_effects=True, vmem_limit_bytes=61 * 2**20
+            collective_id=0, has_side_effects=True, vmem_limit_bytes=56 * 2**20
         ),
         name="hss",
     )(
@@ -541,7 +564,7 @@
             pl.BlockSpec((share, 2 * RANK), lambda i: (0, i)),
         ),
         scratch_shapes=[pltpu.VMEM((2, 128, RANK), F32)],
-        compiler_params=pltpu.CompilerParams(vmem_limit_bytes=61 * 2**20),
+        compiler_params=pltpu.CompilerParams(vmem_limit_bytes=56 * 2**20),
         name="expand",
     )(z, root, nested, inner)
     return basis, nested, approx_t.T

time: 86.3 us -> 84.6 us (0.980)
  Pallas kernels: 84.7 us -> 83.7 us
    pallas_call x1, Pallas kernels: 79.5 us -> 78.5 us  [on_device(): pl.pallas_call(functools.partial(kernel, n_rows), out_shape=(jax.ShapeDty...]
where the time goes in v6:
time: 84.6 us; the launch traced here: 84.4 us
  Pallas kernels  83.7 us (99%)
    pallas_call x1, Pallas kernels, on_device(): pl.pallas_call(functools.partial(kernel, n_rows), out_shape=(jax.ShapeDty...  78.5 us
    pallas_call x1, Pallas kernels, on_device(): pl.pallas_call(outputs, grid=(SAMP // 2,), out_shape=(jax.ShapeDtypeStruc...  5.26 us

profile of v6, /device:TPU:1, one launch (start us, length us, event | category | flops | bytes accessed | tf_op | source)
XLA Modules:
  0.0 84.4 jit_solution(17849908682386187577)
XLA Ops:
  0.6 78.5 %hss.1 = (bf16[8,2,256,256]{3,2,1,0:T(8,128)(2,1)}, bf16[2,256,256]{2,1,0:T(8,128)(2,1)}, f32[256,256]{1,0:T(8,128)}, bf16[2,256,128]{2,1,0:T(8,128)(2,1)}) custom-call(bf16[16,4,128,128]{3,2,1,0:T(8,128)(2,1)} %refs_0_.1, s32[4,16]{1,0:T(4,128)} %bitcast.4, bf16[16,128,512]{2,1,0:T(8,128)(2,1)} %bitcast.3, f32[512,256]{1,0:T(8,128)} %refs_3_.1, ...), custom_call_target="tpu_custom_call" | custom-call | tf_op jit(solution)/shard_map/hss/pallas_call | solution.py:524
  79.1 5.3 %expand.1 = (f32[2048,256]{1,0:T(8,128)}, f32[256,256]{1,0:T(8,128)}, f32[64,2048]{1,0:T(8,128)}) custom-call(bf16[8,2,256,256]{3,2,1,0:T(8,128)(2,1)} %get-tuple-element.10.z_ref, bf16[2,256,256]{2,1,0:T(8,128)(2,1)} %get-tuple-element.11.root_ref, f32[256,256]{1,0:T(8,128)} %get-tuple-element.12.nested_ref, bf16[2,256,128]{2,1,0:T(8,128)(2,1)} %get-tuple-element.13.inner_ref), custom_call_target="tpu_custom_call" | custom-call | tf_op jit(solution)/shard_map/expand/pallas_call | solution.py:547

commit v7 on v6

--- a/solution.py
+++ b/solution.py
@@ -506,15 +506,52 @@
             copy.wait_send()
 
 
-def outputs(z_ref, root_ref, nested_ref, inner_ref, basis_out, nested_out, approx_out, turned):
+OUT_SCRATCH = dict(
+    z=pltpu.VMEM((SAMP, 2, RANK, RANK), BF16),
+    root=pltpu.VMEM((2, RANK, RANK), BF16),
+    inner=pltpu.VMEM((2, RANK, 128), BF16),
+    nested=pltpu.VMEM((RANK, RANK), F32),
+    basis=pltpu.VMEM((SAMP, RANK, RANK), F32),
+    turned=pltpu.VMEM((2, 128, RANK), F32),
+    approx=pltpu.VMEM((64, SAMP * RANK), F32),
+    read=pltpu.SemaphoreType.DMA((SAMP + 3,)),
+    write=pltpu.SemaphoreType.DMA((SAMP + 2,)),
+)
+
+
+def outputs(*refs):
+    z_hbm, root_hbm, nested_hbm, inner_hbm, basis_out, nested_out, approx_out = refs[:7]
+    v = dict(zip(OUT_SCRATCH, refs[7:]))
     core = lax.rem(lax.axis_index("samp"), 2)
-    for i in range(2):
-        rows = pl.ds(256 * i, 256)
-        z = z_ref[i, 0], z_ref[i, 1]
-        basis_out[rows] = dot3(z, (root_ref[0], root_ref[1]))
-        turned[i] = dot3(z, (inner_ref[0], inner_ref[1])).T
-        approx_out[:, rows] = turned[i, pl.ds(pl.multiple_of(core * 64, 64), 64)]
-    nested_out[...] = nested_ref[...]
+    reads = [
+        pltpu.make_async_copy(root_hbm, v["root"], v["read"].at[SAMP]),
+        pltpu.make_async_copy(inner_hbm, v["inner"], v["read"].at[SAMP + 1]),
+    ]
+    blocks = [
+        pltpu.make_async_copy(z_hbm.at[i], v["z"].at[i], v["read"].at[i]) for i in range(SAMP)
+    ]
+    nested_in = pltpu.make_async_copy(nested_hbm, v["nested"], v["read"].at[SAMP + 2])
+    for copy in reads + blocks + [nested_in]:
+        copy.start()
+    for copy in reads:
+        copy.wait()
+    writes = []
+    for i in range(SAMP):
+        blocks[i].wait()
+        rows = pl.ds(RANK * i, RANK)
+        z = v["z"][i, 0], v["z"][i, 1]
+        v["basis"][i] = dot3(z, (v["root"][0], v["root"][1]))
+        writes.append(pltpu.make_async_copy(v["basis"].at[i], basis_out.at[rows], v["write"].at[i]))
+        writes[-1].start()
+        v["turned"][i % 2] = dot3(z, (v["inner"][0], v["inner"][1])).T
+        v["approx"][:, rows] = v["turned"][i % 2, pl.ds(pl.multiple_of(core * 64, 64), 64)]
+    writes.append(pltpu.make_async_copy(v["approx"], approx_out, v["write"].at[SAMP]))
+    writes[-1].start()
+    nested_in.wait()
+    writes.append(pltpu.make_async_copy(v["nested"], nested_out, v["write"].at[SAMP + 1]))
+    writes[-1].start()
+    for copy in writes:
+        copy.wait()
 
 
 def on_device(n_rows, coupling_tiles, tile_columns, sample_matrix, phi_leaf, phi_pair, phi_quad):
@@ -546,24 +583,14 @@
     )
     basis, nested, approx_t = pl.pallas_call(
         outputs,
-        grid=(SAMP // 2,),
         out_shape=(
             jax.ShapeDtypeStruct((rows, RANK), F32),
             jax.ShapeDtypeStruct((RANK, RANK), F32),
             jax.ShapeDtypeStruct((share, rows), F32),
         ),
-        in_specs=[
-            pl.BlockSpec((2, 2, RANK, RANK), lambda i: (i, 0, 0, 0)),
-            pl.BlockSpec((2, RANK, RANK), lambda i: (0, 0, 0)),
-            pl.BlockSpec((RANK, RANK), lambda i: (0, 0)),
-            pl.BlockSpec((2, RANK, 128), lambda i: (0, 0, 0)),
-        ],
-        out_specs=(
-            pl.BlockSpec((2 * RANK, RANK), lambda i: (i, 0)),
-            pl.BlockSpec((RANK, RANK), lambda i: (0, 0)),
-            pl.BlockSpec((share, 2 * RANK), lambda i: (0, i)),
-        ),
-        scratch_shapes=[pltpu.VMEM((2, 128, RANK), F32)],
+        in_specs=[any_] * 4,
+        out_specs=(any_,) * 3,
+        scratch_shapes=list(OUT_SCRATCH.values()),
         compiler_params=pltpu.CompilerParams(vmem_limit_bytes=56 * 2**20),
         name="expand",
     )(z, root, nested, inner)

time: 84.6 us -> 85.3 us (level)
  no operation moved by 1% of the time
where the time goes in v7:
time: 85.3 us; the launch traced here: 85 us
  Pallas kernels  84.2 us (99%)
    pallas_call x1, Pallas kernels, on_device(): pl.pallas_call(functools.partial(kernel, n_rows), out_shape=(jax.ShapeDty...  78.5 us
    pallas_call x1, Pallas kernels, on_device(): pl.pallas_call(outputs, out_shape=(jax.ShapeDtypeStruct((rows, RANK), F32...  5.7 us

profile of v7, /device:TPU:1, one launch (start us, length us, event | category | flops | bytes accessed | tf_op | source)
XLA Modules:
  0.0 85.0 jit_solution(6115149262931015016)
XLA Ops:
  0.6 78.5 %hss.1 = (bf16[8,2,256,256]{3,2,1,0:T(8,128)(2,1)}, bf16[2,256,256]{2,1,0:T(8,128)(2,1)}, f32[256,256]{1,0:T(8,128)}, bf16[2,256,128]{2,1,0:T(8,128)(2,1)}) custom-call(bf16[16,4,128,128]{3,2,1,0:T(8,128)(2,1)} %refs_0_.1, s32[4,16]{1,0:T(4,128)} %bitcast.4, bf16[16,128,512]{2,1,0:T(8,128)(2,1)} %bitcast.3, f32[512,256]{1,0:T(8,128)} %refs_3_.1, ...), custom_call_target="tpu_custom_call" | custom-call | tf_op jit(solution)/shard_map/hss/pallas_call | solution.py:561
  79.1 5.7 %expand.1 = (f32[2048,256]{1,0:T(8,128)}, f32[256,256]{1,0:T(8,128)}, f32[64,2048]{1,0:T(8,128)}) custom-call(bf16[8,2,256,256]{3,2,1,0:T(8,128)(2,1)} %get-tuple-element.10.refs_0_, bf16[2,256,256]{2,1,0:T(8,128)(2,1)} %get-tuple-element.11.refs_1_, f32[256,256]{1,0:T(8,128)} %get-tuple-element.12.refs_2_, bf16[2,256,128]{2,1,0:T(8,128)(2,1)} %get-tuple-element.13.refs_3_), custom_call_target="tpu_custom_call" | custom-call | tf_op jit(solution)/shard_map/expand/pallas_call | solution.py:584

commit v8 on v6

--- a/solution.py
+++ b/solution.py
@@ -13,7 +13,8 @@
 BF16 = jnp.bfloat16
 NT, NN = ((1,), (1,)), ((1,), (0,))
 
-N_COPIES = 96
+N_COPIES = 112
+HANDED = 3
 SAMP = 8
 CHIPS = 4
 RANK = 256
@@ -28,11 +29,11 @@
     phi=pltpu.VMEM((3, 512, 256), F32),
     phi_h=pltpu.VMEM((3, 512, 256), BF16),
     phi_l=pltpu.VMEM((3, 512, 256), BF16),
-    part=pltpu.VMEM((2, 2, 128, 256), F32),
-    code=pltpu.VMEM((6, 256, 256), I16),
-    code_in=pltpu.VMEM((6, 256, 256), I16),
-    unit=pltpu.VMEM((6, 8, 256), F32),
-    unit_in=pltpu.VMEM((6, 8, 256), F32),
+    part=pltpu.VMEM((4, 128, 256), F32),
+    code=pltpu.VMEM((12, 128, 256), I16),
+    code_in=pltpu.VMEM((12, 128, 256), I16),
+    unit=pltpu.VMEM((12, 8, 128), F32),
+    unit_in=pltpu.VMEM((12, 8, 128), F32),
     swap=pltpu.VMEM((256, 256), F32),
     samp=pltpu.VMEM((2, 256, 256), F32),
     mine=pltpu.VMEM((3, 256, 256), F32),
@@ -141,32 +142,35 @@
         copy.start()
         return copy
 
+    def z_at(origin, start=0, size=256):
+        return z_hbm.at[:, pl.ds(pl.multiple_of(256 * origin + start, 128), size)]
+
     mine_half = pl.ds(pl.multiple_of(c * 256, 256), 256)
     own_cols = local(cols_hbm, v["cols"].at[0])
     pl.semaphore_wait(barrier, len(peers))
     with jax.named_scope("halo"):
-        direct = []
-        for i in range(4):
-            at = 4 * x + i
-            piece = b_hbm.at[at, :, mine_half]
-            direct.append(
-                (
-                    remote(piece, v["ext"].at[at], right),
-                    remote(piece, v["ext"].at[32 + at], left),
-                )
+        def to_both(at, count):
+            piece = b_hbm.at[pl.ds(at, count), :, mine_half]
+            return (
+                remote(piece, v["ext"].at[pl.ds(at, count)], right),
+                remote(piece, v["ext"].at[pl.ds(32 + at, count)], left),
             )
+
+        direct = [to_both(4 * x + i, 1) for i in range(HANDED)]
         cols_copy = remote(cols_hbm, v["cols_in"], partner)
-        far = pl.ds(4 * opposite, 4)
+        rest = 4 - HANDED
         far_copies = [
-            remote(b_hbm.at[far, :, mine_half], v["ext"].at[far], right),
-            remote(b_hbm.at[far, :, mine_half], v["ext"].at[pl.ds(32 + 4 * opposite, 4)], left),
+            *to_both(4 * xr + HANDED, rest),
+            *to_both(4 * xl + HANDED, rest),
+            *to_both(4 * x + HANDED, rest),
+            *to_both(4 * opposite, 4),
         ]
         tiles_copy = remote(tiles_hbm, v["tiles"].at[1], partner)
         own_tiles = local(tiles_hbm, v["tiles"].at[0])
         own_b = local(b_hbm.at[:, :, mine_half], v["ext"].at[pl.ds(16, 16)])
         phis = [local(p, v["phi"].at[i]) for i, p in enumerate((phi0_hbm, phi1_hbm, phi2_hbm))]
         handed = []
-        for i in range(4):
+        for i in range(HANDED):
             for side in range(2):
                 direct[i][side].wait_recv()
                 piece = v["ext"].at[32 * side + 4 * x + i]
@@ -185,30 +189,24 @@
             copy.wait_recv()
     first = (r - 1) * 16
 
-    def product(slot, base):
-        def tile_row(t, carry):
-            row = base + t
-            lhs = jnp.concatenate(
-                [v["tiles"][h, row, k] for h in range(2) for k in range(4)], axis=1
-            )
-            rhs = jnp.concatenate(
-                [
-                    v["ext"][jnp.clip(v["cols"][h, k, row] - first, 0, 47)]
-                    for h in range(2)
-                    for k in range(4)
-                ],
-                axis=0,
-            )
-            v["part"][slot, t] = jnp.dot(lhs, rhs, preferred_element_type=F32)
-            return carry
-
-        lax.fori_loop(0, 2, tile_row, 0)
-        return v["part"][slot].reshape(256, 256)
+    def product(row):
+        lhs = jnp.concatenate(
+            [v["tiles"][h, row, k] for h in range(2) for k in range(4)], axis=1
+        )
+        rhs = jnp.concatenate(
+            [
+                v["ext"][jnp.clip(v["cols"][h, k, row] - first, 0, 47)]
+                for h in range(2)
+                for k in range(4)
+            ],
+            axis=0,
+        )
+        return jnp.dot(lhs, rhs, preferred_element_type=F32)
 
     def coded(i, value, device):
         top = jnp.maximum(jnp.max(jnp.abs(value), axis=1, keepdims=True), 1e-30)
         v["code"][i] = jnp.round(value * (32767.0 / top)).astype(jnp.int32).astype(I16)
-        v["unit"][i] = jnp.broadcast_to(top * (1 / 32767.0), (256, 128)).T[0:8]
+        v["unit"][i] = jnp.broadcast_to(top * (1 / 32767.0), (128, 128)).T[0:8]
         return (
             remote(v["code"].at[i], v["code_in"].at[i], device),
             remote(v["unit"].at[i], v["unit_in"].at[i], device),
@@ -217,25 +215,34 @@
     def decoded(i, copies):
         for copy in copies:
             copy.wait_recv()
-        unit = jnp.broadcast_to(v["unit_in"][i, 0:1], (128, 256)).T
+        unit = jnp.broadcast_to(v["unit_in"][i, 0:1], (128, 128)).T
         return v["code_in"][i].astype(jnp.int32).astype(F32) * jnp.concatenate([unit, unit], axis=1)
 
     with jax.named_scope("product"):
-        up_far = coded(0, product(0, 4 * opposite), chip(xr))
-        down_far = coded(1, product(1, 4 * opposite + 2), chip(xl))
-        down_near = coded(2, product(0, 4 * xr + 2), chip(xr))
-        up_near = coded(3, product(1, 4 * xl), chip(xl))
-        up_sum = coded(4, product(0, 4 * xr) + decoded(0, up_far), chip(xr))
-        down_sum = coded(5, product(1, 4 * xl + 2) + decoded(1, down_far), chip(xl))
-        product(0, 4 * x)
-        product(1, 4 * x + 2)
-        upper_in = decoded(3, up_near) + decoded(4, up_sum)
-        lower_in = decoded(2, down_near) + decoded(5, down_sum)
-        upper_half = v["part"][0].reshape(256, 256) + upper_in
-        lower_half = v["part"][1].reshape(256, 256) + lower_in
-        v["swap"][...] = jnp.where(c == 0, lower_half, upper_half)
+        up_far, down_far, up_near, down_near, up_sum, down_sum = ([] for _ in range(6))
+        for j in range(2):
+            up_far.append(coded(j, product(4 * opposite + j), chip(xr)))
+            down_far.append(coded(2 + j, product(4 * opposite + 2 + j), chip(xl)))
+        for j in range(2):
+            down_near.append(coded(4 + j, product(4 * xr + 2 + j), chip(xr)))
+            up_near.append(coded(6 + j, product(4 * xl + j), chip(xl)))
+        for j in range(2):
+            up_sum.append(coded(8 + j, product(4 * xr + j) + decoded(j, up_far[j]), chip(xr)))
+            down_sum.append(
+                coded(10 + j, product(4 * xl + 2 + j) + decoded(2 + j, down_far[j]), chip(xl))
+            )
+        for j in range(4):
+            v["part"][j] = product(4 * x + j)
+        for j in range(2):
+            v["part"][j] = v["part"][j] + decoded(6 + j, up_near[j])
+            v["part"][2 + j] = v["part"][2 + j] + decoded(4 + j, down_near[j])
+        for j in range(2):
+            rows = pl.ds(128 * j, 128)
+            upper = v["part"][j] + decoded(8 + j, up_sum[j])
+            lower = v["part"][2 + j] + decoded(10 + j, down_sum[j])
+            v["swap"][rows] = jnp.where(c == 0, lower, upper)
+            v["samp"][c, rows] = jnp.where(c == 0, upper, lower)
         swapped = remote(v["swap"], v["samp"].at[c], partner)
-        v["samp"][c] = jnp.where(c == 0, upper_half, lower_half)
         swapped.wait_recv()
     def put(slot, value):
         high, low = split(value)
@@ -317,7 +324,7 @@
         v["t_l"][...] = t_low
         v["mine"][0, 0:192] = packed(dot3(transposed(), (v["z_own"][0], v["z_own"][1])))
         sum_g = sum_core(0)
-        z_local = local(v["z_own"], z_hbm.at[s])
+        z_local = local(v["z_own"], z_at(s))
         for half in range(2):
             w = dot3(transposed(), get(half))
             put(3 + half, w)
@@ -427,9 +434,9 @@
         v["t_l"][...] = t_low
         v["swapped_pair"][0, 0:192] = packed(dot3(transposed(), get(0)))
         gram_copy = exchange(0, sibling)
-        z_right = remote(v["z_own"], z_hbm.at[s], chip(xr))
-        z_left = remote(v["z_own"], z_hbm.at[s], chip(xl))
-        z_partner = remote(v["z_own"], z_hbm.at[s], partner)
+        z_right = remote(v["z_own"], z_at(s), chip(xr))
+        z_left = remote(v["z_own"], z_at(s), chip(xl))
+        z_partner = remote(v["z_own"], z_at(s), partner)
         arrived(sum_o)
         put(5, dot3(root(0), split(v["full"][2])) * scale_leaf)
         v["swapped_pair"][1] = dot3(transposed(), get(5))
@@ -468,16 +475,16 @@
         z_right.wait_recv()
         from_left = 2 * xl + c
         round_right = remote(
-            z_hbm.at[from_left, :, 0:128], z_hbm.at[from_left, :, 0:128], chip(xr)
+            z_at(from_left, 0, 128), z_at(from_left, 0, 128), chip(xr)
         )
         z_left.wait_recv()
         from_right = 2 * xr + c
         round_left = remote(
-            z_hbm.at[from_right, :, 128:256], z_hbm.at[from_right, :, 128:256], chip(xl)
+            z_at(from_right, 128, 128), z_at(from_right, 128, 128), chip(xl)
         )
         handed_z = [
-            remote(z_hbm.at[from_left], z_hbm.at[from_left], partner),
-            remote(z_hbm.at[from_right], z_hbm.at[from_right], partner),
+            remote(z_at(from_left), z_at(from_left), partner),
+            remote(z_at(from_right), z_at(from_right), partner),
         ]
         gram_copy = exchange_core(2, gram_copy)
         gram_copy.wait_recv()
@@ -485,7 +492,7 @@
         scale_quad, _, _ = inverse_root(2, unpacked(v["swapped_sum"][2, 0:192]), lambda: None)
         arrived([round_right, round_left])
         from_far = 2 * opposite + c
-        handed_z.append(remote(z_hbm.at[from_far], z_hbm.at[from_far], partner))
+        handed_z.append(remote(z_at(from_far), z_at(from_far), partner))
         nested = dot3(get(4), root(2)) * scale_quad
         v["nested_v"][...] = nested
         nested_copy = local(v["nested_v"], nested_hbm)
@@ -508,12 +515,10 @@
 
 def outputs(z_ref, root_ref, nested_ref, inner_ref, basis_out, nested_out, approx_out, turned):
     core = lax.rem(lax.axis_index("samp"), 2)
-    for i in range(2):
-        rows = pl.ds(256 * i, 256)
-        z = z_ref[i, 0], z_ref[i, 1]
-        basis_out[rows] = dot3(z, (root_ref[0], root_ref[1]))
-        turned[i] = dot3(z, (inner_ref[0], inner_ref[1])).T
-        approx_out[:, rows] = turned[i, pl.ds(pl.multiple_of(core * 64, 64), 64)]
+    z = z_ref[0], z_ref[1]
+    basis_out[...] = dot3(z, (root_ref[0], root_ref[1]))
+    turned[...] = dot3(z, (inner_ref[0], inner_ref[1])).T
+    approx_out[...] = turned[pl.ds(pl.multiple_of(core * 64, 64), 64)]
     nested_out[...] = nested_ref[...]
 
 
@@ -524,7 +529,7 @@
     z, root, nested, inner = pl.pallas_call(
         functools.partial(kernel, n_rows),
         out_shape=(
-            jax.ShapeDtypeStruct((SAMP, 2, RANK, RANK), BF16),
+            jax.ShapeDtypeStruct((2, SAMP * RANK, RANK), BF16),
             jax.ShapeDtypeStruct((2, RANK, RANK), BF16),
             jax.ShapeDtypeStruct((RANK, RANK), F32),
             jax.ShapeDtypeStruct((2, RANK, 128), BF16),
@@ -553,7 +558,7 @@
             jax.ShapeDtypeStruct((share, rows), F32),
         ),
         in_specs=[
-            pl.BlockSpec((2, 2, RANK, RANK), lambda i: (i, 0, 0, 0)),
+            pl.BlockSpec((2, 2 * RANK, RANK), lambda i: (0, i, 0)),
             pl.BlockSpec((2, RANK, RANK), lambda i: (0, 0, 0)),
             pl.BlockSpec((RANK, RANK), lambda i: (0, 0)),
             pl.BlockSpec((2, RANK, 128), lambda i: (0, 0, 0)),
@@ -563,7 +568,7 @@
             pl.BlockSpec((RANK, RANK), lambda i: (0, 0)),
             pl.BlockSpec((share, 2 * RANK), lambda i: (0, i)),
         ),
-        scratch_shapes=[pltpu.VMEM((2, 128, RANK), F32)],
+        scratch_shapes=[pltpu.VMEM((128, 2 * RANK), F32)],
         compiler_params=pltpu.CompilerParams(vmem_limit_bytes=56 * 2**20),
         name="expand",
     )(z, root, nested, inner)

time: 84.6 us -> 84.9 us (level); the launches traced: 84.4 us -> 83.6 us
  Pallas kernels: 83.7 us -> 82.8 us
    pallas_call x1, Pallas kernels: 78.5 us -> 77.5 us  [on_device(): pl.pallas_call(functools.partial(kernel, n_rows), out_shape=(jax.ShapeDty...]
where the time goes in v8:
time: 84.9 us; the launch traced here: 83.6 us
  Pallas kernels  82.8 us (98%)
    pallas_call x1, Pallas kernels, on_device(): pl.pallas_call(functools.partial(kernel, n_rows), out_shape=(jax.ShapeDty...  77.5 us
    pallas_call x1, Pallas kernels, on_device(): pl.pallas_call(outputs, grid=(SAMP // 2,), out_shape=(jax.ShapeDtypeStruc...  5.34 us

profile of v8, /device:TPU:1, one launch (start us, length us, event | category | flops | bytes accessed | tf_op | source)
XLA Modules:
  0.0 83.6 jit_solution(9563958586418456450)
XLA Ops:
  0.6 77.5 %hss.1 = (bf16[2,2048,256]{2,1,0:T(8,128)(2,1)}, bf16[2,256,256]{2,1,0:T(8,128)(2,1)}, f32[256,256]{1,0:T(8,128)}, bf16[2,256,128]{2,1,0:T(8,128)(2,1)}) custom-call(bf16[16,4,128,128]{3,2,1,0:T(8,128)(2,1)} %refs_0_.1, s32[4,16]{1,0:T(4,128)} %bitcast.4, bf16[16,128,512]{2,1,0:T(8,128)(2,1)} %bitcast.3, f32[512,256]{1,0:T(8,128)} %refs_3_.1, ...), custom_call_target="tpu_custom_call" | custom-call | tf_op jit(solution)/shard_map/hss/pallas_call | solution.py:529
  78.1 5.3 %expand.1 = (f32[2048,256]{1,0:T(8,128)}, f32[256,256]{1,0:T(8,128)}, f32[64,2048]{1,0:T(8,128)}) custom-call(bf16[2,2048,256]{2,1,0:T(8,128)(2,1)} %get-tuple-element.10.z_ref, bf16[2,256,256]{2,1,0:T(8,128)(2,1)} %get-tuple-element.11.root_ref, f32[256,256]{1,0:T(8,128)} %get-tuple-element.12.nested_ref, bf16[2,256,128]{2,1,0:T(8,128)(2,1)} %get-tuple-element.13.inner_ref), custom_call_target="tpu_custom_call" | custom-call | tf_op jit(solution)/shard_map/expand/pallas_call | solution.py:552

commit v9 on v8

--- a/solution.py
+++ b/solution.py
@@ -14,7 +14,6 @@
 NT, NN = ((1,), (1,)), ((1,), (0,))
 
 N_COPIES = 112
-HANDED = 3
 SAMP = 8
 CHIPS = 4
 RANK = 256
@@ -156,21 +155,15 @@
                 remote(piece, v["ext"].at[pl.ds(32 + at, count)], left),
             )
 
-        direct = [to_both(4 * x + i, 1) for i in range(HANDED)]
+        direct = [to_both(4 * x + i, 1) for i in range(4)]
         cols_copy = remote(cols_hbm, v["cols_in"], partner)
-        rest = 4 - HANDED
-        far_copies = [
-            *to_both(4 * xr + HANDED, rest),
-            *to_both(4 * xl + HANDED, rest),
-            *to_both(4 * x + HANDED, rest),
-            *to_both(4 * opposite, 4),
-        ]
+        far_copies = to_both(4 * opposite, 4)
         tiles_copy = remote(tiles_hbm, v["tiles"].at[1], partner)
         own_tiles = local(tiles_hbm, v["tiles"].at[0])
         own_b = local(b_hbm.at[:, :, mine_half], v["ext"].at[pl.ds(16, 16)])
         phis = [local(p, v["phi"].at[i]) for i, p in enumerate((phi0_hbm, phi1_hbm, phi2_hbm))]
         handed = []
-        for i in range(HANDED):
+        for i in range(4):
             for side in range(2):
                 direct[i][side].wait_recv()
                 piece = v["ext"].at[32 * side + 4 * x + i]
@@ -185,7 +178,7 @@
         other_cols = local(v["cols_in"], v["cols"].at[1])
         for copy in (own_cols, own_tiles, own_b, other_cols):
             copy.wait()
-        for copy in [tiles_copy] + far_copies + handed:
+        for copy in [tiles_copy, *far_copies, *handed]:
             copy.wait_recv()
     first = (r - 1) * 16
 
@@ -551,24 +544,24 @@
     )
     basis, nested, approx_t = pl.pallas_call(
         outputs,
-        grid=(SAMP // 2,),
+        grid=(SAMP // 4,),
         out_shape=(
             jax.ShapeDtypeStruct((rows, RANK), F32),
             jax.ShapeDtypeStruct((RANK, RANK), F32),
             jax.ShapeDtypeStruct((share, rows), F32),
         ),
         in_specs=[
-            pl.BlockSpec((2, 2 * RANK, RANK), lambda i: (0, i, 0)),
+            pl.BlockSpec((2, 4 * RANK, RANK), lambda i: (0, i, 0)),
             pl.BlockSpec((2, RANK, RANK), lambda i: (0, 0, 0)),
             pl.BlockSpec((RANK, RANK), lambda i: (0, 0)),
             pl.BlockSpec((2, RANK, 128), lambda i: (0, 0, 0)),
         ],
         out_specs=(
-            pl.BlockSpec((2 * RANK, RANK), lambda i: (i, 0)),
+            pl.BlockSpec((4 * RANK, RANK), lambda i: (i, 0)),
             pl.BlockSpec((RANK, RANK), lambda i: (0, 0)),
-            pl.BlockSpec((share, 2 * RANK), lambda i: (0, i)),
+            pl.BlockSpec((share, 4 * RANK), lambda i: (0, i)),
         ),
-        scratch_shapes=[pltpu.VMEM((128, 2 * RANK), F32)],
+        scratch_shapes=[pltpu.VMEM((128, 4 * RANK), F32)],
         compiler_params=pltpu.CompilerParams(vmem_limit_bytes=56 * 2**20),
         name="expand",
     )(z, root, nested, inner)

time: 84.9 us -> 83.5 us (0.984); the launches traced: 83.6 us -> 83.4 us
  no operation moved by 1% of the time
where the time goes in v9:
time: 83.5 us; the launch traced here: 83.4 us
  Pallas kernels  82.6 us (99%)
    pallas_call x1, Pallas kernels, on_device(): pl.pallas_call(functools.partial(kernel, n_rows), out_shape=(jax.ShapeDty...  78 us
    pallas_call x1, Pallas kernels, on_device(): pl.pallas_call(outputs, grid=(SAMP // 4,), out_shape=(jax.ShapeDtypeStruc...  4.62 us

profile of v9, /device:TPU:1, one launch (start us, length us, event | category | flops | bytes accessed | tf_op | source)
XLA Modules:
  0.0 83.4 jit_solution(14695165831397047590)
XLA Ops:
  0.6 78.0 %hss.1 = (bf16[2,2048,256]{2,1,0:T(8,128)(2,1)}, bf16[2,256,256]{2,1,0:T(8,128)(2,1)}, f32[256,256]{1,0:T(8,128)}, bf16[2,256,128]{2,1,0:T(8,128)(2,1)}) custom-call(bf16[16,4,128,128]{3,2,1,0:T(8,128)(2,1)} %refs_0_.1, s32[4,16]{1,0:T(4,128)} %bitcast.4, bf16[16,128,512]{2,1,0:T(8,128)(2,1)} %bitcast.3, f32[512,256]{1,0:T(8,128)} %refs_3_.1, ...), custom_call_target="tpu_custom_call" | custom-call | tf_op jit(solution)/shard_map/hss/pallas_call | solution.py:522
  78.7 4.6 %expand.1 = (f32[2048,256]{1,0:T(8,128)}, f32[256,256]{1,0:T(8,128)}, f32[64,2048]{1,0:T(8,128)}) custom-call(bf16[2,2048,256]{2,1,0:T(8,128)(2,1)} %get-tuple-element.10.z_ref, bf16[2,256,256]{2,1,0:T(8,128)(2,1)} %get-tuple-element.11.root_ref, f32[256,256]{1,0:T(8,128)} %get-tuple-element.12.nested_ref, bf16[2,256,128]{2,1,0:T(8,128)(2,1)} %get-tuple-element.13.inner_ref), custom_call_target="tpu_custom_call" | custom-call | tf_op jit(solution)/shard_map/expand/pallas_call | solution.py:545

commit v10 on v9

--- a/solution.py
+++ b/solution.py
@@ -411,14 +411,14 @@
     with jax.named_scope("leaf"):
 
         def last_sums():
-            last_n, last_o = sum_last(1, sum_n), sum_last(2, sum_o)
+            last_n = sum_last(1, sum_n)
             columns = [
                 remote(v["w_chip"].at[d], v["w_in"].at[o], chip(d))
                 for o, d in enumerate((xr, opposite, xl))
             ]
-            return last_n, last_o, columns
-
-        scale_leaf, x_leaf, (sum_n, sum_o, w_copies) = inverse_root(0, unpacked(v["full"][0, 0:192]), last_sums)
+            return last_n, columns
+
+        scale_leaf, x_leaf, (sum_n, w_copies) = inverse_root(0, unpacked(v["full"][0, 0:192]), last_sums)
         arrived(sum_n)
         zp = dot3(root(0), split(v["full"][1])) * scale_leaf
         put(0, zp)
@@ -427,6 +427,7 @@
         v["t_l"][...] = t_low
         v["swapped_pair"][0, 0:192] = packed(dot3(transposed(), get(0)))
         gram_copy = exchange(0, sibling)
+        sum_o = sum_last(2, sum_o)
         z_right = remote(v["z_own"], z_at(s), chip(xr))
         z_left = remote(v["z_own"], z_at(s), chip(xl))
         z_partner = remote(v["z_own"], z_at(s), partner)

time: 83.5 us -> 82.8 us (level)
  the two profiles are of different devices: /device:TPU:1 before, /device:TPU:17 now
where the time goes in v10:
time: 82.8 us; the launch traced here: 82.7 us
  Pallas kernels  81.9 us (99%)
    pallas_call x1, Pallas kernels, on_device(): pl.pallas_call(functools.partial(kernel, n_rows), out_shape=(jax.ShapeDty...  77.3 us
    pallas_call x1, Pallas kernels, on_device(): pl.pallas_call(outputs, grid=(SAMP // 4,), out_shape=(jax.ShapeDtypeStruc...  4.63 us

profile of v10, /device:TPU:17, one launch (start us, length us, event | category | flops | bytes accessed | tf_op | source)
XLA Modules:
  0.0 82.7 jit_solution(14613584216036282107)
XLA Ops:
  0.6 77.3 %hss.1 = (bf16[2,2048,256]{2,1,0:T(8,128)(2,1)}, bf16[2,256,256]{2,1,0:T(8,128)(2,1)}, f32[256,256]{1,0:T(8,128)}, bf16[2,256,128]{2,1,0:T(8,128)(2,1)}) custom-call(bf16[16,4,128,128]{3,2,1,0:T(8,128)(2,1)} %refs_0_.1, s32[4,16]{1,0:T(4,128)} %bitcast.4, bf16[16,128,512]{2,1,0:T(8,128)(2,1)} %bitcast.3, f32[512,256]{1,0:T(8,128)} %refs_3_.1, ...), custom_call_target="tpu_custom_call" | custom-call | tf_op jit(solution)/shard_map/hss/pallas_call | solution.py:523
  77.9 4.6 %expand.1 = (f32[2048,256]{1,0:T(8,128)}, f32[256,256]{1,0:T(8,128)}, f32[64,2048]{1,0:T(8,128)}) custom-call(bf16[2,2048,256]{2,1,0:T(8,128)(2,1)} %get-tuple-element.10.z_ref, bf16[2,256,256]{2,1,0:T(8,128)(2,1)} %get-tuple-element.11.root_ref, f32[256,256]{1,0:T(8,128)} %get-tuple-element.12.nested_ref, bf16[2,256,128]{2,1,0:T(8,128)(2,1)} %get-tuple-element.13.inner_ref), custom_call_target="tpu_custom_call" | custom-call | tf_op jit(solution)/shard_map/expand/pallas_call | solution.py:546
